TPU v7x, 1024 devices: a whole 4x4x32 slice. The times are simulated.
1024 devices in a mesh: seq: 64 (over z, y_hi), chan: 16 (over y_lo, x, core).
Axes of the slice: x: 4, y: 4 (y_hi: 2, y_lo: 2; y = y_hi * 2 + y_lo), z: 32, core: 2. Of those that a mesh axis runs over, the one named last changes fastest.
Arguments:
- tokens: bfloat16 [16384, 4096], P('seq', 'chan'), may hold values from -6 to 6
- w_in: bfloat16 [4096, 3, 4096], P(None, None, 'chan'), may hold values from -0.09375 to 0.09375
- short_filter: float32 [3, 3, 4096], P(None, None, 'chan'), may hold values from -3 to 3
- mr_filter: bfloat16 [256, 128], P('chan'), may hold values from -0.5 to 0.5
- skip_gain: float32 [4096], P('chan'), may hold values from -4 to 4
- w_out: bfloat16 [4096, 4096], P('chan'), may hold values from -0.09375 to 0.09375
- segments: int32 [16384], replicated, may hold values from 0 to 15, never falling along the last dimension, each value on 1 to 2048 neighbouring positions
Outputs:
- mixed: bfloat16 [16384, 4096], P('seq', 'chan')
Inputs may be any that keep to these rules, and one draw needn't show every extreme that they name: `segments`: document ids in contiguous sequence order never fall; each of the 16 documents holds 1 to 2048 positions and one holds exactly that many.
All inputs are finite; a program needn't handle non-finite values.
Results may differ from a plain program's by a relative error of at most 0.0076.
Values may be sent and summed in bfloat16 or wider, within the bound.
No kernel may reach another device: no remote copies, remote signals or barrier semaphores. Data moves between devices by JAX's collectives and lax.ppermute only.
A program may use at most 64 MiB of HBM per device.

v0:
```python
import jax
import jax.numpy as jnp
from jax import lax
from jax.sharding import PartitionSpec as P


def from_behind(value, axis, steps):
    count = lax.axis_size(axis)
    first, last = (max(0, -steps), min(count, count - steps))
    return lax.ppermute(value, axis, [(source, source + steps) for source in range(first, last)])


def short_conv(extended, seg_ext, weights):
    short_taps = weights.shape[0]
    row_count = extended.shape[0] - short_taps + 1
    seg_own = seg_ext[short_taps - 1 :]
    tail_shape = (row_count,) + (1,) * (extended.ndim - 1)
    running = jnp.zeros((row_count,) + extended.shape[1:], jnp.float32)
    for tap_index in range(short_taps):
        lead_rows = short_taps - 1 - tap_index
        shifted = extended[lead_rows : lead_rows + row_count].astype(jnp.float32)
        same_doc = (seg_ext[lead_rows : lead_rows + row_count] == seg_own).astype(jnp.float32)
        running = running + weights[tap_index] * shifted * same_doc.reshape(tail_shape)
    return running


def band_matrix(filters):
    groups, tap_count = filters.shape
    flipped = filters[:, ::-1]
    blank = jnp.zeros((groups, tap_count), filters.dtype)
    row_pattern = jnp.concatenate([blank, flipped, blank], axis=1)
    tiled_rows = jnp.tile(row_pattern, (1, tap_count))
    tiled_rows = jnp.concatenate([tiled_rows, blank], axis=1)
    shaped = tiled_rows.reshape(groups, tap_count, 3 * tap_count + 1)[:, :, : 2 * tap_count]
    return shaped[:, ::-1, :]


def long_conv(gated_ext, band_mats, seg_gated, seg_own):
    groups, tap_count = (band_mats.shape[0], band_mats.shape[1])
    row_count = seg_own.shape[0]
    block_count = row_count // tap_count
    blocks = gated_ext.reshape(block_count + 1, tap_count, groups, -1)
    window = jnp.concatenate([blocks[:-1], blocks[1:]], axis=1)
    seg_blocks = seg_gated.reshape(block_count + 1, tap_count)
    seg_window = jnp.concatenate([seg_blocks[:-1], seg_blocks[1:]], axis=1)
    doc_mask = seg_own.reshape(block_count, tap_count)[:, :, None] == seg_window[:, None, :]
    masked = jnp.where(doc_mask[:, None], band_mats[None], jnp.zeros((), band_mats.dtype))
    result = jnp.einsum("ngab,nbgc->nagc", masked, window, preferred_element_type=jnp.float32)
    return result.reshape(row_count, -1)


def body(tokens, w_in, short_filter, mr_filter, skip_gain, w_out, segments):
    row_count = tokens.shape[0]
    model_width = w_in.shape[0]
    chan_count = w_in.shape[2]
    seq_count = lax.axis_size("seq")
    tap_count = mr_filter.shape[1]
    short_taps = short_filter.shape[0]
    halo_rows = tap_count + short_taps - 1
    flat_in = w_in.reshape(model_width, 3 * chan_count)
    projected = jnp.dot(
        lax.all_gather(tokens, "chan", axis=1, tiled=True),
        flat_in,
        preferred_element_type=jnp.float32,
    )
    qkv = projected.astype(jnp.bfloat16)
    periods = row_count // (2 * seq_count)
    sendable = qkv.reshape(seq_count, periods, 2, 3, chan_count)
    received = lax.all_to_all(sendable, "seq", split_axis=0, concat_axis=0, tiled=True)
    first_slot = jnp.swapaxes(received[:, :, 0], 0, 1)
    second = jnp.swapaxes(received[::-1, :, 1], 0, 1)
    contiguous = jnp.concatenate([first_slot, second], axis=1).reshape(row_count, 3, chan_count)
    base_row = lax.axis_index("seq") * row_count
    seg_padded = jnp.concatenate([jnp.full((halo_rows,), -1, jnp.int32), segments])
    seg_ext = lax.dynamic_slice_in_dim(seg_padded, base_row, row_count + halo_rows, 0)
    query_tail = contiguous[row_count - (short_taps - 1) :, 0]
    pair_tail = contiguous[row_count - halo_rows :, 1:3]
    query_prev, pair_prev = from_behind((query_tail, pair_tail), "seq", 1)
    query_ext = jnp.concatenate([query_prev, contiguous[:, 0]])
    pair_ext = jnp.concatenate([pair_prev, contiguous[:, 1:3]])
    query_conv = short_conv(query_ext, seg_ext[tap_count:], short_filter[:, 0])
    pair_conv = short_conv(pair_ext, seg_ext, short_filter[:, 1:3])
    gated_ext = (pair_conv[:, 0] * pair_conv[:, 1]).astype(jnp.bfloat16)
    gated_local = gated_ext[tap_count:]
    band_mats = band_matrix(mr_filter)
    group_count = mr_filter.shape[0]
    long_out = long_conv(
        gated_ext.reshape(tap_count + row_count, group_count, -1),
        band_mats,
        seg_ext[short_taps - 1 :],
        seg_ext[halo_rows:],
    )
    gated_out = (query_conv * (long_out + skip_gain * gated_local.astype(jnp.float32))).astype(
        jnp.bfloat16
    )
    period_parts = gated_out.reshape(periods, 2, seq_count, chan_count)
    stacked = jnp.stack([period_parts[:, 0], period_parts[:, 1, ::-1]], axis=2)
    outgoing = jnp.swapaxes(stacked, 0, 1)
    returned = lax.all_to_all(outgoing, "seq", split_axis=0, concat_axis=0, tiled=True)
    folded_out = returned.reshape(row_count, chan_count)
    summed = lax.psum_scatter(
        lax.dot_general(
            w_out, folded_out, (((0,), (1,)), ((), ())), preferred_element_type=jnp.float32
        ),
        "chan",
        scatter_dimension=0,
        tiled=True,
    )
    return summed.T.astype(jnp.bfloat16)


def solution(mesh):
    return jax.shard_map(
        body,
        mesh=mesh,
        in_specs=(
            P("seq", "chan"),
            P(None, None, "chan"),
            P(None, None, "chan"),
            P("chan", None),
            P("chan"),
            P("chan", None),
            P(),
        ),
        out_specs=P("seq", "chan"),
        check_vma=False,
    )
```

profile of v0, /device:TPU:1, one launch (start us, length us, event | category | flops | bytes accessed | tf_op | source)
XLA Modules:
  0.0 292.0 jit_solution(11675352141243840292)
XLA Ops:
  7.3 8.8 %copy.33 = bf16[4096,3,256]{0,2,1:T(8,128)(2,1)} copy(bf16[4096,3,256]{2,0,1:T(8,128)(2,1)} %param.8) | data formatting | bytes 12582912 | tf_op args[1]
  16.0 57.7 %all-gather.2.cloned.1.call-done = bf16[256,4096]{1,0:T(8,128)(2,1)} async-done(((bf16[256,256]{1,0:T(8,128)(2,1)}), bf16[256,4096]{1,0:T(8,128)(2,1)}) %all-gather.2.cloned.1.call-update) | async-done | bytes 2097168 | tf_op jit(solution)/shard_map/all_gather | solution.py:62
  73.7 5.3 %convolution_convert_fusion = bf16[256,768]{1,0:T(8,128)(2,1)S(1)} fusion(bf16[256,4096]{1,0:T(8,128)(2,1)} %all-gather.2.cloned.1.call-done, bf16[4096,768]{0,1:T(8,128)(2,1)} %bitcast.63), kind=kOutput, calls=%fused_computation.4 | convolution fusion | flops 1610809344 | bytes 8781824 | tf_op jit(solution)/shard_map/dot_general | solution.py:61
  79.2 1.1 copy.34
  80.3 25.3 %all-to-all-start = ((bf16[64,2,2,3,256]{4,2,3,1,0:T(2,128)(2,1)}), bf16[64,2,2,3,256]{4,2,3,1,0:T(2,128)(2,1)S(1)}, u32[]{:S(2)}, u32[]{:S(2)}) async-start(bf16[64,2,2,3,256]{4,2,3,1,0:T(2,128)(2,1)} %copy.34), calls=%async_computation | async-start | bytes 786432 | tf_op jit(solution)/shard_map/all_to_all | solution.py:69
  105.9 0.9 copy.51
  106.8 1.2 concatenate.31
  108.0 5.7 %reshape.66 = bf16[16,128,385]{2,1,0:T(8,128)(2,1)} reshape(bf16[16,49280]{1,0:T(8,128)(2,1)} %concatenate.31) | data formatting | bytes 3153920 | tf_op jit(solution)/shard_map/reshape | solution.py:34
  113.7 1.2 slice-done
  114.9 10.1 %rev.14 = bf16[16,128,256]{2,1,0:T(8,128)(2,1)} reverse(bf16[16,128,256]{2,1,0:T(8,128)(2,1)S(1)} %slice-done), dimensions={1} | reverse | bytes 2097152 | tf_op jit(solution)/shard_map/rev | solution.py:35
  126.6 1.3 fusion.24
  127.9 1.3 slice_bitcast_fusion.5
  129.9 28.7 %all-to-all-done = bf16[64,2,2,3,256]{4,2,3,1,0:T(2,128)(2,1)S(1)} async-done(((bf16[64,2,2,3,256]{4,2,3,1,0:T(2,128)(2,1)}), bf16[64,2,2,3,256]{4,2,3,1,0:T(2,128)(2,1)S(1)}, u32[]{:S(2)}, u32[]{:S(2)}) %all-to-all-start) | async-done | bytes 393248 | tf_op jit(solution)/shard_map/all_to_all | solution.py:69
  160.1 3.4 %collective-permute-start.1 = (bf16[130,2,256]{2,0,1:T(8,128)(2,1)S(1)}, bf16[130,2,256]{2,0,1:T(8,128)(2,1)S(1)}, u32[]{:S(2)}, u32[]{:S(2)}) collective-permute-start(bf16[130,2,256]{2,0,1:T(8,128)(2,1)S(1)} %slice.172), channel_id=1, source_target_pairs={{0,16},{16,32},{32,48},{48,64},{64,80},{80,96},{96,112},{112,128},... | collective-permute-start | bytes 399368 | tf_op jit(solution)/shard_map/ppermute | solution.py:10
  163.5 2.6 collective-permute-start
  167.9 1.0 copy.37
  169.6 1.6 copy.39
  171.1 1.0 copy.38
  172.8 0.9 copy.40
  173.8 1.6 fusion.3
  177.1 36.8 %all_to_all.10 = bf16[64,2,2,256]{3,1,2,0:T(2,128)(2,1)S(1)} all-to-all(bf16[64,2,2,256]{3,1,2,0:T(2,128)(2,1)S(1)} %copy.45), channel_id=1, replica_groups=mesh['seq'=64,'chan'=16] {'seq'}, dimensions={0} | all-to-all | bytes 262144 | tf_op jit(solution)/shard_map/all_to_all | solution.py:99
  214.1 2.7 convolution_bitcast_fusion
  216.8 66.8 %reduce-scatter.2.cloned.1.call-done = f32[256,256]{0,1:T(8,128)} async-done(((f32[4096,256]{0,1:T(8,128)}), f32[256,256]{0,1:T(8,128)}) %reduce-scatter.2.cloned.1.call-update) | async-done | bytes 262160 | tf_op jit(solution)/shard_map/reduce_scatter | solution.py:101
  283.5 1.6 convert_bitcast_fusion
  (62 shorter events, 9.9 us)
Async XLA Ops:
  6.5 207.5 %copy-start = (bf16[256,4096]{1,0:T(8,128)(2,1)S(1)}, bf16[256,4096]{1,0:T(8,128)(2,1)}, u32[]{:S(2)}) copy-start(bf16[256,4096]{1,0:T(8,128)(2,1)} %param.12) | copy-start | bytes 6291460
  6.5 67.2 %all-gather.2.cloned.1.call-start = ((), (), s32[]{:S(2)}) async-start(), calls=%async_computation.3 | async-start | bytes 2228224 | tf_op jit(solution)/shard_map/all_gather | solution.py:62
  79.0 26.6 %copy-start.5 = (bf16[16,128]{1,0:T(8,128)(2,1)S(1)}, bf16[16,128]{1,0:T(8,128)(2,1)}, u32[]{:S(2)}) copy-start(bf16[16,128]{1,0:T(8,128)(2,1)} %param.10) | copy-start | bytes 12292
  80.3 78.3 %all-to-all-start = ((bf16[64,2,2,3,256]{4,2,3,1,0:T(2,128)(2,1)}), bf16[64,2,2,3,256]{4,2,3,1,0:T(2,128)(2,1)S(1)}, u32[]{:S(2)}, u32[]{:S(2)}) async-start(bf16[64,2,2,3,256]{4,2,3,1,0:T(2,128)(2,1)} %copy.34), calls=%async_computation | async-start | bytes 786432 | tf_op jit(solution)/shard_map/all_to_all | solution.py:69
  105.6 178.0 %reduce-scatter.2.cloned.1.call-start = ((), (), s32[]{:S(2)}) async-start(), calls=%async_computation.4 | async-start | bytes 4456448 | tf_op jit(solution)/shard_map/reduce_scatter | solution.py:101
  113.7 1.2 slice-start
  159.2 7.6 %copy-start.4 = (f32[2,256]{1,0:T(2,128)S(1)}, f32[2,256]{1,0:T(2,128)}, u32[]{:S(2)}) copy-start(f32[2,256]{1,0:T(2,128)} %get-tuple-element.16) | copy-start | bytes 6148
  160.1 6.6 %collective-permute-start.1 = (bf16[130,2,256]{2,0,1:T(8,128)(2,1)S(1)}, bf16[130,2,256]{2,0,1:T(8,128)(2,1)S(1)}, u32[]{:S(2)}, u32[]{:S(2)}) collective-permute-start(bf16[130,2,256]{2,0,1:T(8,128)(2,1)S(1)} %slice.172), channel_id=1, source_target_pairs={{0,16},{16,32},{32,48},{48,64},{64,80},{80,96},{96,112},{112,128},... | collective-permute-start | bytes 399368 | tf_op jit(solution)/shard_map/ppermute | solution.py:10
  163.5 12.3 %collective-permute-start = (bf16[2,256]{1,0:T(2,128)(2,1)}, bf16[2,256]{1,0:T(2,128)(2,1)}, u32[]{:S(2)}, u32[]{:S(2)}) collective-permute-start(bf16[2,256]{1,0:T(2,128)(2,1)} %slice_bitcast_fusion.6), channel_id=1, source_target_pairs={{0,16},{16,32},{32,48},{48,64},{64,80},{80,96},{96,112},{112,128},... | collective-permute-start | bytes 3080 | tf_op jit(solution)/shard_map/ppermute | solution.py:10
  166.8 7.0 %copy-start.1 = (bf16[16,128,256]{2,1,0:T(8,128)(2,1)S(1)}, bf16[16,128,256]{2,1,0:T(8,128)(2,1)}, u32[]{:S(2)}) copy-start(bf16[16,128,256]{2,1,0:T(8,128)(2,1)} %rev.14) | copy-start | bytes 3145732
  166.8 7.0 %copy-start.3 = (pred[2,128,256]{2,1,0:T(8,128)(4,1)S(1)}, pred[2,128,256]{2,1,0:T(8,128)(4,1)}, u32[]{:S(2)}) copy-start(pred[2,128,256]{2,1,0:T(8,128)(4,1)} %broadcast_compare_fusion) | copy-start | bytes 196612
  173.8 2.0 copy-start.2
  173.8 2.0 copy-start.6
  173.8 2.0 copy-start.7
  173.8 2.0 copy-start.8
  173.8 2.0 copy-start.9
Sparse Core Ops, SparseCore 0:
  10.0 63.7 all-gather.1
  216.9 66.5 reduce-scatter.1
where the time goes:
time: 293 us; the launch traced here: 292 us
  waiting for transfers between devices  154 us (53%)
  local copies, waits for them, and re-layouts  42.4 us (14%)
  blocking collectives  36.8 us (13%)
  starting transfers between devices  31.3 us (11%)
  between operations  13.7 us (5%)
  matrix products  9.49 us (3%)
  other arithmetic  4.44 us (2%)
    reduce_scatter x1, waiting for transfers between devices, body(): lax.psum_scatter(lax.dot_general(w_out, folded_out, (((0,), (1,)), ((), (...  66.8 us
    all_gather x1, waiting for transfers between devices, body(): lax.all_gather(tokens, 'chan', axis=1, tiled=True)  57.7 us
    all_to_all x1, blocking collectives, body(): lax.all_to_all(outgoing, 'seq', split_axis=0, concat_axis=0, tiled=True)  36.8 us
    all_to_all x1, waiting for transfers between devices, body(): lax.all_to_all(sendable, 'seq', split_axis=0, concat_axis=0, tiled=True)  28.7 us
    all_to_all x1, starting transfers between devices, body(): lax.all_to_all(sendable, 'seq', split_axis=0, concat_axis=0, tiled=True)  25.3 us
    rev x1, local copies, waits for them, and re-layouts, band_matrix(): return shaped[:, ::-1, :]  10.1 us
    unnamed x25, local copies, waits for them, and re-layouts  9.79 us
    slice x7, local copies, waits for them, and re-layouts, long_conv(): window = jnp.concatenate([blocks[:-1], blocks[1:]], axis=1)  6.6 us
  transfers between devices with their start and end apart: 5, of which 3 were waited for; matrix products, arithmetic and copies ran while one was open for 14% of the time, Pallas kernels for 0%

commit v1 on v0

v1 whole, which is shorter than its diff:
```python
import functools

import jax
import jax.numpy as jnp
from jax import lax
from jax.experimental import pallas as pl
from jax.experimental.pallas import tpu as pltpu
from jax.sharding import PartitionSpec as P

BF16 = jnp.bfloat16
F32 = jnp.float32


def iota(shape, dim):
    return lax.broadcasted_iota(jnp.int32, shape, dim)


def dot(a, b):
    return jnp.dot(a, b, preferred_element_type=F32)


def cost(flops, moved):
    return pl.CostEstimate(flops=flops, bytes_accessed=moved, transcendentals=0)


def fold_source(position, seq_count):
    period, phase = position // (2 * seq_count), position % (2 * seq_count)
    late = phase >= seq_count
    device = jnp.where(late, 2 * seq_count - 1 - phase, phase)
    return device, 2 * period + late.astype(jnp.int32)


def unfold_kernel(seq_count, received, spread):
    copies, rows, lanes = spread.shape
    half = received.shape[1]
    device, slot = fold_source(iota((rows, received.shape[0]), 0), seq_count)
    column = iota((rows, received.shape[0]), 1)
    data = received[...]
    for part in range(lanes // half):
        pick = (column == device * 8 + part * 4 + slot).astype(BF16)
        moved = dot(pick, data).astype(BF16)
        for copy in range(copies):
            spread[copy, :, part * half : (part + 1) * half] = moved


def refold_kernel(seq_count, terms, outgoing):
    half = outgoing.shape[1]
    rows = terms.shape[1]
    total = terms[0].astype(F32)
    for term in range(1, terms.shape[0]):
        total = total + terms[term].astype(F32)
    mixed = total.astype(BF16)
    shape = (outgoing.shape[0], rows)
    device, slot = fold_source(iota(shape, 1), seq_count)
    target = iota(shape, 0)
    moved = None
    for part in range(terms.shape[2] // half):
        pick = (target == device * 8 + part * 4 + slot).astype(BF16)
        term = dot(pick, mixed[:, part * half : (part + 1) * half])
        moved = term if moved is None else moved + term
    outgoing[...] = moved.astype(BF16)


def project_first_kernel(core, rows, weights, total):
    @pl.when(pl.program_id(0) == 0)
    def _():
        total[...] = jnp.zeros_like(total)

    accumulate(rows, weights, total)


def accumulate(rows, weights, total):
    for block in range(rows.shape[0]):
        for part in range(total.shape[0]):
            total[part] += dot(rows[block], weights[part, block])


def segment_columns(segments, first, count):
    blocks = []
    for block in range(count):
        row = segments[pl.ds(first + block, 1), :].astype(F32)
        blocks.append(jnp.transpose(jnp.broadcast_to(row, (128, 128))))
    return jnp.concatenate(blocks, axis=0)


def short_conv(extended, columns, taps, lead):
    own = columns[lead:, :1]
    result = taps[0] * extended[lead:]
    for tap in range(1, taps.shape[0]):
        shifted = pltpu.roll(extended, tap, 0)[lead:]
        same = (pltpu.roll(columns, tap, 0)[lead:, :1] == own).astype(F32)
        result = result + taps[tap] * shifted * same
    return result


def project_last_kernel(scalars, rows, weights, partial, segments, short_filter, qkv, halo, total):
    step = pl.program_id(0)

    @pl.when(step == 0)
    def _():
        total[...] = partial[...]

    accumulate(rows, weights, total)

    @pl.when(step == pl.num_programs(0) - 1)
    def _():
        count = qkv.shape[1]
        for part in range(3):
            rounded = total[part].astype(BF16)
            qkv[part] = rounded
            halo[128 + 16 * part : 144 + 16 * part, :] = rounded[count - 16 :]
        columns = segment_columns(segments, 2 * scalars[1], 2)[count - 136 :]
        pair = []
        for part in (1, 2):
            extended = qkv[part].astype(F32)[count - 136 :]
            taps = jnp.stack([short_filter[tap, part : part + 1, :] for tap in range(3)])
            pair.append(short_conv(extended, columns, taps, 8))
        halo[:128, :] = (pair[0] * pair[1]).astype(BF16)


def band_kernel(filters, bands):
    groups, taps = filters.shape
    flip = iota((taps, 2 * taps), 1) == taps - iota((taps, 2 * taps), 0)
    first_rows = dot(filters[...], flip.astype(BF16))
    for group in range(groups):
        row = jnp.broadcast_to(first_rows[group : group + 1], (taps, 2 * taps))
        bands[group] = pltpu.roll(row, 0, 1, stride=1, stride_axis=0).astype(BF16)


def mix_kernel(scalars, qkv, halo, bands, segments, short_filter, skip_gain, gated_out):
    seq = scalars[1]
    count, chans = gated_out.shape
    groups = bands.shape[0]
    size = chans // groups
    ahead = segment_columns(segments, jnp.maximum(2 * seq - 1, 0), 1)
    ahead = jnp.where(seq > 0, ahead, -1.0)
    columns = jnp.concatenate([ahead, segment_columns(segments, 2 * seq, 2)], axis=0)
    convolved = []
    for part in range(3):
        lead = halo[128 + 16 * part : 144 + 16 * part, :].astype(F32)[8:]
        extended = jnp.concatenate([lead, qkv[part].astype(F32)], axis=0)
        taps = jnp.stack([short_filter[tap, part : part + 1, :] for tap in range(3)])
        convolved.append(short_conv(extended, columns[120:], taps, 8))
    gated = (convolved[1] * convolved[2]).astype(BF16)
    gated_ext = jnp.concatenate([halo[:128, :], gated], axis=0)
    lane_group = iota((256, 128), 1) // size
    for block in range(count // 128):
        own = columns[128 * (block + 1) : 128 * (block + 2)]
        masks = [
            (own == jnp.transpose(columns[128 * (block + k) : 128 * (block + k + 1)]))
            for k in range(2)
        ]
        mask = jnp.concatenate(masks, axis=1).astype(F32).astype(BF16)
        for side in range(chans // 128):
            lanes = slice(128 * side, 128 * (side + 1))
            window = gated_ext[128 * block : 128 * block + 256, lanes]
            total = jnp.zeros((128, 128), F32)
            for group in range(128 // size):
                band = bands[side * (128 // size) + group] * mask
                chosen = jnp.where(lane_group == group, window, jnp.zeros((), BF16))
                total = total + dot(band, chosen)
            rows = slice(128 * block, 128 * (block + 1))
            direct = skip_gain[:, lanes] * gated[rows, lanes].astype(F32)
            gated_out[rows, lanes] = (convolved[0][rows, lanes] * (total + direct)).astype(BF16)


def out_kernel(core, rows, weights, sums):
    sums[0] = dot(rows[...], weights[...]).astype(sums.dtype)


def whole(shape):
    return pl.BlockSpec(shape, lambda *_: (0,) * len(shape))


def body(tokens, w_in, short_filter, mr_filter, skip_gain, w_out, segments):
    rows, chans = tokens.shape
    width = w_in.shape[0]
    seq_count = lax.axis_size("seq")
    chan_count = lax.axis_size("chan")
    chips = chan_count // 2
    core = lax.axis_index("chan") % 2
    seq = lax.axis_index("seq")
    scalars = jnp.stack([core, seq]).astype(jnp.int32)
    same_core = [[2 * chip + c for chip in range(chips)] for c in range(2)]
    partners = [(i, i ^ 1) for i in range(chan_count)]
    segments = segments.reshape(-1, 128)
    gain = skip_gain.reshape(1, chans)
    half = chans // 2

    sendable = tokens.reshape(seq_count, 4, 2, half).swapaxes(1, 2).reshape(seq_count, 8, half)
    received = lax.all_to_all(sendable, "seq", 0, 0, tiled=True)
    spread = pl.pallas_call(
        functools.partial(unfold_kernel, seq_count),
        out_shape=jax.ShapeDtypeStruct((chips, rows, chans), BF16),
        cost_estimate=cost(4 * rows * rows * chans, 2 * (chips + 1) * rows * chans),
        name="unfold",
    )(received.reshape(seq_count * 8, half))
    near = lax.all_to_all(spread, "chan", 0, 0, axis_index_groups=same_core, tiled=True)
    far = lax.ppermute(near, "chan", partners)

    weights = w_in.transpose(1, 0, 2).reshape(3, chips, 2, chans, chans)
    project_cost = cost(3 * rows * width * chans, 3 * width * chans)
    steps = 4
    per = chips // steps
    rows_spec = pl.BlockSpec((per, rows, chans), lambda i, s: (i, 0, 0))
    total_spec = pl.BlockSpec((3, rows, chans), lambda i, s: (0, 0, 0))
    partial = pl.pallas_call(
        project_first_kernel,
        out_shape=jax.ShapeDtypeStruct((3, rows, chans), F32),
        grid_spec=pltpu.PrefetchScalarGridSpec(
            num_scalar_prefetch=1,
            grid=(steps,),
            in_specs=[
                rows_spec,
                pl.BlockSpec((3, per, None, chans, chans), lambda i, s: (0, i, s[0], 0, 0)),
            ],
            out_specs=total_spec,
        ),
        cost_estimate=project_cost,
        name="project_first",
    )(scalars, near, weights)
    bands = pl.pallas_call(
        band_kernel,
        out_shape=jax.ShapeDtypeStruct((mr_filter.shape[0], 128, 256), BF16),
        cost_estimate=cost(1 << 20, 1 << 21),
        name="bands",
    )(mr_filter)
    qkv, halo = pl.pallas_call(
        project_last_kernel,
        out_shape=(
            jax.ShapeDtypeStruct((3, rows, chans), BF16),
            jax.ShapeDtypeStruct((176, chans), BF16),
        ),
        grid_spec=pltpu.PrefetchScalarGridSpec(
            num_scalar_prefetch=1,
            grid=(steps,),
            in_specs=[
                rows_spec,
                pl.BlockSpec((3, per, None, chans, chans), lambda i, s: (0, i, 1 - s[0], 0, 0)),
                total_spec,
                whole(segments.shape),
                whole(short_filter.shape),
            ],
            out_specs=(total_spec, whole((176, chans))),
            scratch_shapes=[pltpu.VMEM((3, rows, chans), F32)],
        ),
        cost_estimate=project_cost,
        name="project_last",
    )(scalars, far, weights, partial, segments, short_filter)

    before = lax.ppermute(halo, "seq", [(i, i + 1) for i in range(seq_count - 1)])
    gated_out = pl.pallas_call(
        mix_kernel,
        out_shape=jax.ShapeDtypeStruct((rows, chans), BF16),
        grid_spec=pltpu.PrefetchScalarGridSpec(
            num_scalar_prefetch=1,
            grid=(1,),
            in_specs=[
                whole(qkv.shape),
                whole(before.shape),
                whole(bands.shape),
                whole(segments.shape),
                whole(short_filter.shape),
                whole(gain.shape),
            ],
            out_specs=whole((rows, chans)),
        ),
        cost_estimate=cost(1 << 29, 1 << 21),
        name="mix",
    )(scalars, qkv, before, bands, segments, short_filter, gain)

    def out_sums(other, dtype, name):
        return pl.pallas_call(
            out_kernel,
            out_shape=jax.ShapeDtypeStruct((chips, rows, chans), dtype),
            grid_spec=pltpu.PrefetchScalarGridSpec(
                num_scalar_prefetch=1,
                grid=(chips,),
                in_specs=[
                    whole((rows, chans)),
                    pl.BlockSpec(
                        (chans, chans), lambda i, s: (0, 2 * i + (1 - s[0] if other else s[0]))
                    ),
                ],
                out_specs=pl.BlockSpec((1, rows, chans), lambda i, s: (i, 0, 0)),
            ),
            cost_estimate=cost(rows * width * chans, width * chans),
            name=name,
        )(scalars, gated_out, w_out)

    given = lax.ppermute(out_sums(True, BF16, "out_other"), "chan", partners)
    kept = out_sums(False, F32, "out_own")
    pair = (kept + given.astype(F32)).astype(BF16)
    terms = lax.all_to_all(pair, "chan", 0, 0, axis_index_groups=same_core, tiled=True)
    outgoing = pl.pallas_call(
        functools.partial(refold_kernel, seq_count),
        out_shape=jax.ShapeDtypeStruct((seq_count * 8, half), BF16),
        cost_estimate=cost(4 * rows * rows * chans, 2 * (chips + 1) * rows * chans),
        name="refold",
    )(terms)
    returned = lax.all_to_all(outgoing.reshape(seq_count, 8, half), "seq", 0, 0, tiled=True)
    return returned.reshape(seq_count, 2, 4, half).swapaxes(1, 2).reshape(rows, chans)


def solution(mesh):
    return jax.shard_map(
        body,
        mesh=mesh,
        in_specs=(
            P("seq", "chan"),
            P(None, None, "chan"),
            P(None, None, "chan"),
            P("chan", None),
            P("chan"),
            P("chan", None),
            P(),
        ),
        out_specs=P("seq", "chan"),
        check_vma=False,
    )
```

time: 293 us -> 193 us (0.66)
  waiting for transfers between devices: 154 us -> 0.13 us
  blocking collectives: 36.8 us -> 136 us
  local copies, waits for them, and re-layouts: 42.4 us -> 3.37 us
  Pallas kernels: 0 us -> 34.9 us
  starting transfers between devices: 31.3 us -> 13.7 us
  between operations: 13.7 us -> 0.06 us
  matrix products: 9.49 us -> 0 us
    all_to_all x1 -> x4, blocking collectives: 36.8 us -> 136 us  [the longest x1 62.5 us: body(): received = lax.all_to_all(sendable, 'seq', 0, 0, tiled=True)]
    reduce_scatter x1 -> x0, waiting for transfers between devices: 66.8 us -> none  [body(): lax.psum_scatter(lax.dot_general(w_out, folded_out, (((0,), (1,)), ((), (...]
    all_gather x1 -> x0, waiting for transfers between devices: 57.7 us -> none  [body(): lax.all_gather(tokens, 'chan', axis=1, tiled=True)]
    pallas_call x0 -> x8, Pallas kernels: none -> 34.9 us  [the longest x2 13.4 us: out_sums(): pl.pallas_call(out_kernel, out_shape=jax.ShapeDtypeStruct((chips, rows, c...]
    all_to_all x1 -> x0, waiting for transfers between devices: 28.7 us -> none  [body(): lax.all_to_all(sendable, 'seq', split_axis=0, concat_axis=0, tiled=True)]
    all_to_all x1 -> x0, starting transfers between devices: 25.3 us -> none  [body(): lax.all_to_all(sendable, 'seq', split_axis=0, concat_axis=0, tiled=True)]
    rev x4 -> x0, local copies, waits for them, and re-layouts: 10.5 us -> none  [the longest x1 10.1 us: band_matrix(): return shaped[:, ::-1, :]]
    slice x14 -> x0, local copies, waits for them, and re-layouts: 9.8 us -> none  [the longest x7 6.6 us: long_conv(): window = jnp.concatenate([blocks[:-1], blocks[1:]], axis=1)]
  transfers between devices with their start and end apart: 5 -> 3, of which waited for: 3 -> 1; matrix products, arithmetic and copies ran while one was open for 14% -> 0% of each run, Pallas kernels for 0% -> 7%
where the time goes in v1:
time: 193 us; the launch traced here: 190 us
  blocking collectives  136 us (70%)
  Pallas kernels  34.9 us (18%)
  starting transfers between devices  13.7 us (7%)
  local copies, waits for them, and re-layouts  3.37 us (2%)
  other arithmetic  2.42 us (1%)
    all_to_all x1, blocking collectives, body(): received = lax.all_to_all(sendable, 'seq', 0, 0, tiled=True)  62.5 us
    all_to_all x1, blocking collectives, body(): lax.all_to_all(outgoing.reshape(seq_count, 8, half), 'seq', 0, 0, tiled=T...  38.8 us
    all_to_all x1, blocking collectives, body(): lax.all_to_all(pair, 'chan', 0, 0, axis_index_groups=same_core, tiled=True)  18.7 us
    all_to_all x1, blocking collectives, body(): lax.all_to_all(spread, 'chan', 0, 0, axis_index_groups=same_core, tiled=T...  15.9 us
    pallas_call x2, Pallas kernels, out_sums(): pl.pallas_call(out_kernel, out_shape=jax.ShapeDtypeStruct((chips, rows, c...  13.4 us
    ppermute x1, starting transfers between devices, body(): far = lax.ppermute(near, 'chan', partners)  6.8 us
    pallas_call x1, Pallas kernels, body(): pl.pallas_call(project_last_kernel, out_shape=(jax.ShapeDtypeStruct((3, r...  5.72 us
    pallas_call x1, Pallas kernels, body(): pl.pallas_call(project_first_kernel, out_shape=jax.ShapeDtypeStruct((3, r...  5.31 us
  transfers between devices with their start and end apart: 3, of which 1 were waited for; matrix products, arithmetic and copies ran while one was open for 0% of the time, Pallas kernels for 7%

profile of v1, /device:TPU:1, one launch (start us, length us, event | category | flops | bytes accessed | tf_op | source)
XLA Modules:
  0.0 190.4 jit_solution(6620136019098859387)
XLA Ops:
  0.0 0.9 reshape.27
  1.0 62.5 %all_to_all.20 = bf16[64,8,128]{2,1,0:T(8,128)(2,1)} all-to-all(bf16[64,8,128]{2,1,0:T(8,128)(2,1)S(1)} %bitcast.22), channel_id=1, replica_groups=mesh['seq'=64,'chan'=16] {'seq'}, dimensions={0} | all-to-all | bytes 262144 | tf_op jit(solution)/shard_map/all_to_all | solution.py:191
  63.5 2.2 %unfold.1 = bf16[8,256,256]{2,1,0:T(8,128)(2,1)} custom-call(bf16[512,128]{1,0:T(8,128)(2,1)} %bitcast.20), custom_call_target="tpu_custom_call" | custom-call | flops 67108864 | bytes 1179648 | tf_op jit(solution)/shard_map/unfold/pallas_call | solution.py:192
  65.7 15.9 %all_to_all.21.rows = bf16[8,256,256]{2,1,0:T(8,128)(2,1)S(1)} all-to-all(bf16[8,256,256]{2,1,0:T(8,128)(2,1)} %unfold.1), channel_id=1, replica_groups={{0,2,4,6,8,10,12,14},{1,3,5,7,9,11,13,15},{16,18,20,22,24,26,28,30},{17..., dimensions={0} | all-to-all | bytes 2097152 | tf_op jit(solution)/shard_map/all_to_all | solution.py:198
  81.6 6.8 %collective-permute-start = (bf16[8,256,256]{2,1,0:T(8,128)(2,1)S(1)}, bf16[8,256,256]{2,1,0:T(8,128)(2,1)S(1)}, u32[]{:S(2)}, u32[]{:S(2)}) collective-permute-start(bf16[8,256,256]{2,1,0:T(8,128)(2,1)S(1)} %all_to_all.21.rows), channel_id=1, source_target_pairs={{0,1},{1,0},{2,3},{3,2},{4,5},{5,4},{6,7},{7,6},{8,9},{9,8},{10,11... | collective-permute-start | bytes 3145736 | tf_op jit(solution)/shard_map/ppermute | solution.py:199
  88.4 0.6 pad_add_fusion.core.scalars
  89.0 5.3 %project_first.1.partial = f32[3,256,256]{2,1,0:T(8,128)} custom-call(s32[2]{0:T(128)} %pad_add_fusion.core.scalars, bf16[8,256,256]{2,1,0:T(8,128)(2,1)} %copy-done, bf16[3,8,2,256,256]{4,3,2,1,0:T(8,128)(2,1)} %bitcast.18), custom_call_target="tpu_custom_call" | custom-call | flops 805306368 | bytes 3145728 | tf_op jit(solution)/shard_map/project_first/pallas_call | solution.py:207
  94.3 0.0 collective-permute-done.rows
  94.3 1.0 copy-done.1
  95.3 5.7 %project_last.1 = (bf16[3,256,256]{2,1,0:T(8,128)(2,1)}, bf16[176,256]{1,0:T(8,128)(2,1)}) custom-call(s32[2]{0:T(128)} %pad_add_fusion.core.scalars, bf16[8,256,256]{2,1,0:T(8,128)(2,1)} %copy-done.1, bf16[3,8,2,256,256]{4,3,2,1,0:T(8,128)(2,1)} %bitcast.19, f32[3,256,256]{2,1,0:T(8,128)} %project_first.1.partial, s32[128,128]{1,0:T(8,128)} %bitcast.26, ...), custom_call_target="tpu_custom_call" | custom-call | flops 805306368 | bytes 3145728 | tf_op jit(solution)/shard_map/project_last/pallas_call | solution.py:228
  101.0 4.1 %collective-permute-start.1 = (bf16[176,256]{1,0:T(8,128)(2,1)}, bf16[176,256]{1,0:T(8,128)(2,1)S(1)}, u32[]{:S(2)}, u32[]{:S(2)}) collective-permute-start(bf16[176,256]{1,0:T(8,128)(2,1)} %get-tuple-element.8), channel_id=1, source_target_pairs={{0,16},{16,32},{32,48},{48,64},{64,80},{80,96},{96,112},{112,128},... | collective-permute-start | bytes 270344 | tf_op jit(solution)/shard_map/ppermute | solution.py:251
  105.1 2.1 %bands.1 = bf16[16,128,256]{2,1,0:T(8,128)(2,1)} custom-call(bf16[16,128]{1,0:T(8,128)(2,1)} %filters.1), custom_call_target="tpu_custom_call" | custom-call | flops 1048576 | bytes 2097152 | tf_op jit(solution)/shard_map/bands/pallas_call | solution.py:222
  107.3 0.1 collective-permute-done.1.halo
  107.4 0.6 copy-done.2
  108.0 3.8 %mix.1.rows = bf16[256,256]{1,0:T(8,128)(2,1)} custom-call(s32[2]{0:T(128)} %pad_add_fusion.core.scalars, bf16[3,256,256]{2,1,0:T(8,128)(2,1)} %get-tuple-element.7.qkv, bf16[176,256]{1,0:T(8,128)(2,1)} %copy-done.2, bf16[16,128,256]{2,1,0:T(8,128)(2,1)} %bands.1, s32[128,128]{1,0:T(8,128)} %bitcast.27, f32[3,3,256]{2,1,0:T(4,128)} %short_filter.3, ...), custom_call_target="tpu_custom_call" | custom-call | flops 536870912 | bytes 2097152 | tf_op jit(solution)/shard_map/mix/pallas_call | solution.py:252
  111.8 6.6 %out_other.1 = bf16[8,256,256]{2,1,0:T(8,128)(2,1)} custom-call(s32[2]{0:T(128)} %pad_add_fusion.core.scalars, bf16[256,256]{1,0:T(8,128)(2,1)} %mix.1.rows, bf16[256,4096]{1,0:T(8,128)(2,1)} %weights.3), custom_call_target="tpu_custom_call" | custom-call | flops 268435456 | bytes 1048576 | tf_op jit(solution)/shard_map/out_other/pallas_call | solution.py:273
  118.4 2.8 %collective-permute-start.2 = (bf16[8,256,256]{2,1,0:T(8,128)(2,1)}, bf16[8,256,256]{2,1,0:T(8,128)(2,1)S(1)}, u32[]{:S(2)}, u32[]{:S(2)}) collective-permute-start(bf16[8,256,256]{2,1,0:T(8,128)(2,1)} %out_other.1), channel_id=1, source_target_pairs={{0,1},{1,0},{2,3},{3,2},{4,5},{5,4},{6,7},{7,6},{8,9},{9,8},{10,11... | collective-permute-start | bytes 3145736 | tf_op jit(solution)/shard_map/ppermute | solution.py:291
  121.2 6.8 %out_own.1 = f32[8,256,256]{2,1,0:T(8,128)} custom-call(s32[2]{0:T(128)} %pad_add_fusion.core.scalars, bf16[256,256]{1,0:T(8,128)(2,1)} %mix.1.rows, bf16[256,4096]{1,0:T(8,128)(2,1)} %weights.3), custom_call_target="tpu_custom_call" | custom-call | flops 268435456 | bytes 1048576 | tf_op jit(solution)/shard_map/out_own/pallas_call | solution.py:273
  128.0 1.8 add_convert_fusion
  129.8 18.7 %all_to_all.22.terms = bf16[8,256,256]{2,1,0:T(8,128)(2,1)} all-to-all(bf16[8,256,256]{2,1,0:T(8,128)(2,1)S(1)} %add_convert_fusion), channel_id=1, replica_groups={{0,2,4,6,8,10,12,14},{1,3,5,7,9,11,13,15},{16,18,20,22,24,26,28,30},{17..., dimensions={0} | all-to-all | bytes 2097152 | tf_op jit(solution)/shard_map/all_to_all | solution.py:294
  148.6 2.3 %refold.1 = bf16[512,128]{1,0:T(8,128)(2,1)} custom-call(bf16[8,256,256]{2,1,0:T(8,128)(2,1)} %all_to_all.22.terms), custom_call_target="tpu_custom_call" | custom-call | flops 67108864 | bytes 1179648 | tf_op jit(solution)/shard_map/refold/pallas_call | solution.py:295
  150.9 38.8 %all_to_all.23 = bf16[64,8,128]{2,1,0:T(8,128)(2,1)S(1)} all-to-all(bf16[64,8,128]{2,1,0:T(8,128)(2,1)} %bitcast.21), channel_id=1, replica_groups=mesh['seq'=64,'chan'=16] {'seq'}, dimensions={0} | all-to-all | bytes 262144 | tf_op jit(solution)/shard_map/all_to_all | solution.py:301
  189.6 0.1 copy.9
  189.7 0.7 copy.12
  (6 shorter events, 0.1 us)
Async XLA Ops:
  81.6 7.4 %copy-start = (bf16[8,256,256]{2,1,0:T(8,128)(2,1)}, bf16[8,256,256]{2,1,0:T(8,128)(2,1)S(1)}, u32[]{:S(2)}) copy-start(bf16[8,256,256]{2,1,0:T(8,128)(2,1)S(1)} %all_to_all.21.rows) | copy-start | bytes 3145732
  81.6 12.7 %collective-permute-start = (bf16[8,256,256]{2,1,0:T(8,128)(2,1)S(1)}, bf16[8,256,256]{2,1,0:T(8,128)(2,1)S(1)}, u32[]{:S(2)}, u32[]{:S(2)}) collective-permute-start(bf16[8,256,256]{2,1,0:T(8,128)(2,1)S(1)} %all_to_all.21.rows), channel_id=1, source_target_pairs={{0,1},{1,0},{2,3},{3,2},{4,5},{5,4},{6,7},{7,6},{8,9},{9,8},{10,11... | collective-permute-start | bytes 3145736 | tf_op jit(solution)/shard_map/ppermute | solution.py:199
  94.3 1.0 copy-start.1
  101.0 6.4 %collective-permute-start.1 = (bf16[176,256]{1,0:T(8,128)(2,1)}, bf16[176,256]{1,0:T(8,128)(2,1)S(1)}, u32[]{:S(2)}, u32[]{:S(2)}) collective-permute-start(bf16[176,256]{1,0:T(8,128)(2,1)} %get-tuple-element.8), channel_id=1, source_target_pairs={{0,16},{16,32},{32,48},{48,64},{64,80},{80,96},{96,112},{112,128},... | collective-permute-start | bytes 270344 | tf_op jit(solution)/shard_map/ppermute | solution.py:251
  107.4 0.6 copy-start.2
  118.4 9.6 %collective-permute-start.2 = (bf16[8,256,256]{2,1,0:T(8,128)(2,1)}, bf16[8,256,256]{2,1,0:T(8,128)(2,1)S(1)}, u32[]{:S(2)}, u32[]{:S(2)}) collective-permute-start(bf16[8,256,256]{2,1,0:T(8,128)(2,1)} %out_other.1), channel_id=1, source_target_pairs={{0,1},{1,0},{2,3},{3,2},{4,5},{5,4},{6,7},{7,6},{8,9},{9,8},{10,11... | collective-permute-start | bytes 3145736 | tf_op jit(solution)/shard_map/ppermute | solution.py:291

commit v2 on v1

v2 whole, which is shorter than its diff:
```python
import functools

import jax
import jax.numpy as jnp
from jax import lax
from jax.experimental import pallas as pl
from jax.experimental.pallas import tpu as pltpu
from jax.sharding import PartitionSpec as P

BF16 = jnp.bfloat16
F32 = jnp.float32
SEQ = 64


def iota(shape, dim):
    return lax.broadcasted_iota(jnp.int32, shape, dim)


def dot(a, b):
    return jnp.dot(a, b, preferred_element_type=F32)


def cost(flops, moved):
    return pl.CostEstimate(flops=flops, bytes_accessed=moved, transcendentals=0)


def params(mib):
    return pltpu.CompilerParams(vmem_limit_bytes=mib << 20)


def block_of(device):
    z, half = device // 2, device % 2
    return jnp.where(half == 0, z, SEQ - 1 - z)


def fold_source(position):
    period, phase = position // (2 * SEQ), position % (2 * SEQ)
    late = phase >= SEQ
    return jnp.where(late, 2 * SEQ - 1 - phase, phase), 2 * period + late.astype(jnp.int32)


def pack_kernel(tokens, packed):
    shape = (packed.shape[0], tokens.shape[0])
    target, source = iota(shape, 0), iota(shape, 1)
    wanted = 4 * block_of(target // 8) + target % 4
    moved = None
    for part in range(2):
        pick = (source == wanted) & (target // 4 % 2 == part)
        term = dot(pick.astype(BF16), tokens[:, 128 * part : 128 * (part + 1)])
        moved = term if moved is None else moved + term
    packed[...] = moved.astype(BF16)


def unpack_kernel(packed, rows):
    shape = (rows.shape[0], packed.shape[0])
    target, source = iota(shape, 0), iota(shape, 1)
    for part in range(2):
        wanted = (block_of(source // 8) == target // 4) & (source % 8 == 4 * part + target % 4)
        moved = dot(wanted.astype(BF16), packed[...])
        rows[:, 128 * part : 128 * (part + 1)] = moved.astype(BF16)


def unfold_kernel(received, spread):
    copies, rows, _ = spread.shape
    shape = (rows, received.shape[0])
    device, slot = fold_source(iota(shape, 0))
    column = iota(shape, 1)
    for part in range(2):
        pick = (column == device * 8 + part * 4 + slot).astype(BF16)
        moved = dot(pick, received[...]).astype(BF16)
        for copy in range(copies):
            spread[copy, :, 128 * part : 128 * (part + 1)] = moved


def refold_kernel(terms, outgoing):
    total = terms[0].astype(F32)
    for term in range(1, terms.shape[0]):
        total = total + terms[term].astype(F32)
    mixed = total.astype(BF16)
    shape = (outgoing.shape[0], mixed.shape[0])
    device, slot = fold_source(iota(shape, 1))
    target = iota(shape, 0)
    moved = None
    for part in range(2):
        pick = (target == device * 8 + part * 4 + slot).astype(BF16)
        term = dot(pick, mixed[:, 128 * part : 128 * (part + 1)])
        moved = term if moved is None else moved + term
    outgoing[...] = moved.astype(BF16)


def segment_columns(segments, first, count):
    blocks = []
    for block in range(count):
        row = segments[pl.ds(first + block, 1), :].astype(F32)
        blocks.append(jnp.transpose(jnp.broadcast_to(row, (128, 128))))
    return jnp.concatenate(blocks, axis=0)


def short_conv(extended, columns, taps, lead):
    own = columns[lead:, :1]
    result = taps[0] * extended[lead:]
    for tap in range(1, taps.shape[0]):
        shifted = pltpu.roll(extended, tap, 0)[lead:]
        same = (pltpu.roll(columns, tap, 0)[lead:, :1] == own).astype(F32)
        result = result + taps[tap] * shifted * same
    return result


def project(other, rows, weights, fetched, sems, finish):
    chips, _, width = rows.shape
    core = lax.axis_index("chan") % 2
    parity = 1 - core if other else core
    copies = [
        pltpu.make_async_copy(weights.at[part, :, parity], fetched.at[part], sems.at[part])
        for part in range(3)
    ]
    for copy in copies:
        copy.start()
    data = jnp.concatenate([rows[chip] for chip in range(chips)], axis=1)
    for part in range(3):
        copies[part].wait()
        finish(part, dot(data, fetched[part].reshape(chips * width, width)))


def project_near_kernel(rows, weights, partial, fetched, sems):
    def finish(part, total):
        partial[part] = total

    project(False, rows, weights, fetched, sems, finish)


def project_far_kernel(rows, weights, partial, segments, short_filter, qkv, halo, fetched, sems):
    count = qkv.shape[1]

    def finish(part, total):
        rounded = (partial[part] + total).astype(BF16)
        qkv[part] = rounded
        halo[128 + 16 * part : 144 + 16 * part, :] = rounded[count - 16 :]

    project(True, rows, weights, fetched, sems, finish)
    block = block_of(lax.axis_index("seq"))
    columns = segment_columns(segments, 2 * block, 2)[count - 136 :]
    pair = []
    for part in (1, 2):
        extended = qkv[part].astype(F32)[count - 136 :]
        taps = jnp.stack([short_filter[tap, part : part + 1, :] for tap in range(3)])
        pair.append(short_conv(extended, columns, taps, 8))
    halo[:128, :] = (pair[0] * pair[1]).astype(BF16)


def band_kernel(filters, bands):
    groups, taps = filters.shape
    flip = iota((taps, 2 * taps), 1) == taps - iota((taps, 2 * taps), 0)
    first_rows = dot(filters[...], flip.astype(BF16))
    for group in range(groups):
        row = jnp.broadcast_to(first_rows[group : group + 1], (taps, 2 * taps))
        bands[group] = pltpu.roll(row, 0, 1, stride=1, stride_axis=0).astype(BF16)


def mix_kernel(qkv, halo, bands, segments, short_filter, skip_gain, gated_out):
    seq = block_of(lax.axis_index("seq"))
    count, chans = gated_out.shape
    groups = bands.shape[0]
    size = chans // groups
    ahead = segment_columns(segments, jnp.maximum(2 * seq - 1, 0), 1)
    ahead = jnp.where(seq > 0, ahead, -1.0)
    columns = jnp.concatenate([ahead, segment_columns(segments, 2 * seq, 2)], axis=0)
    convolved = []
    for part in range(3):
        lead = halo[128 + 16 * part : 144 + 16 * part, :].astype(F32)[8:]
        extended = jnp.concatenate([lead, qkv[part].astype(F32)], axis=0)
        taps = jnp.stack([short_filter[tap, part : part + 1, :] for tap in range(3)])
        convolved.append(short_conv(extended, columns[120:], taps, 8))
    gated = (convolved[1] * convolved[2]).astype(BF16)
    gated_ext = jnp.concatenate([halo[:128, :], gated], axis=0)
    lane_group = iota((256, 128), 1) // size
    for block in range(count // 128):
        own = columns[128 * (block + 1) : 128 * (block + 2)]
        masks = [
            (own == jnp.transpose(columns[128 * (block + k) : 128 * (block + k + 1)]))
            for k in range(2)
        ]
        mask = jnp.concatenate(masks, axis=1).astype(F32).astype(BF16)
        for side in range(chans // 128):
            lanes = slice(128 * side, 128 * (side + 1))
            window = gated_ext[128 * block : 128 * block + 256, lanes]
            total = jnp.zeros((128, 128), F32)
            for group in range(128 // size):
                band = bands[side * (128 // size) + group] * mask
                chosen = jnp.where(lane_group == group, window, jnp.zeros((), BF16))
                total = total + dot(band, chosen)
            rows = slice(128 * block, 128 * (block + 1))
            direct = skip_gain[:, lanes] * gated[rows, lanes].astype(F32)
            gated_out[rows, lanes] = (convolved[0][rows, lanes] * (total + direct)).astype(BF16)


def out_kernel(other, rows, weights, sums):
    core = lax.axis_index("chan") % 2
    parity = 1 - core if other else core
    chips, _, width = sums.shape
    for chip in range(chips):
        columns = pl.ds(pl.multiple_of((2 * chip + parity) * width, width), width)
        sums[chip] = dot(rows[...], weights[:, columns]).astype(sums.dtype)


def kernel(body, name, out_shape, mib, flops, moved, in_place=(), scratch=()):
    vector = pl.BlockSpec(memory_space=pltpu.VMEM)
    anywhere = pl.BlockSpec(memory_space=pltpu.HBM)

    def call(*args):
        return pl.pallas_call(
            body,
            out_shape=out_shape,
            in_specs=[anywhere if i in in_place else vector for i in range(len(args))],
            out_specs=jax.tree.map(lambda _: vector, out_shape),
            scratch_shapes=scratch,
            compiler_params=params(mib),
            cost_estimate=cost(flops, moved),
            name=name,
        )(*args)

    return call


def array(shape, dtype=BF16):
    return jax.ShapeDtypeStruct(shape, dtype)


def body(tokens, w_in, short_filter, mr_filter, skip_gain, w_out, segments):
    rows, chans = tokens.shape
    width = w_in.shape[0]
    chan_count = lax.axis_size("chan")
    chips = chan_count // 2
    same_core = [[2 * chip + c for chip in range(chips)] for c in range(2)]
    partners = [(i, i ^ 1) for i in range(chan_count)]
    holder = {int(k): d for d, k in enumerate([d // 2 if d % 2 == 0 else SEQ - 1 - d // 2 for d in range(SEQ)])}
    ahead = [(holder[k], holder[k + 1]) for k in range(SEQ - 1)]
    segments = segments.reshape(-1, 128)
    gain = skip_gain.reshape(1, chans)
    moved = rows * chans * 2

    packed = kernel(pack_kernel, "pack", array((8 * SEQ, 128)), 4, 1 << 26, 2 * moved)(tokens)
    received = lax.all_to_all(packed.reshape(SEQ, 8, 128), "seq", 0, 0, tiled=True)
    spread = kernel(unfold_kernel, "unfold", array((chips, rows, chans)), 8, 1 << 27, 9 * moved)(
        received.reshape(8 * SEQ, 128)
    )
    near = lax.all_to_all(spread, "chan", 0, 0, axis_index_groups=same_core, tiled=True)
    far = lax.ppermute(near, "chan", partners)
    bands = kernel(band_kernel, "bands", array((mr_filter.shape[0], 128, 256)), 8, 1 << 24, 8 * moved)(mr_filter)
    weights = w_in.transpose(1, 0, 2).reshape(3, chips, 2, chans, chans)
    work = 3 * rows * width * chans
    scratch = [pltpu.VMEM((3, chips, chans, chans), BF16), pltpu.SemaphoreType.DMA((3,))]
    partial = kernel(
        project_near_kernel, "project_near", array((3, rows, chans), F32), 51, work, 40 * moved, (1,), scratch
    )(near, weights)
    qkv, halo = kernel(
        project_far_kernel,
        "project_far",
        (array((3, rows, chans)), array((176, chans))),
        51,
        work,
        40 * moved,
        (1,),
        scratch,
    )(far, weights, partial, segments, short_filter)

    before = lax.ppermute(halo, "seq", ahead)
    gated_out = kernel(mix_kernel, "mix", array((rows, chans)), 8, 1 << 29, 16 * moved)(
        qkv, before, bands, segments, short_filter, gain
    )

    def out_sums(other, dtype, name):
        return kernel(
            functools.partial(out_kernel, other),
            name,
            array((chips, rows, chans), dtype),
            8,
            rows * width * chans,
            16 * moved,
        )(gated_out, w_out)

    given = lax.ppermute(out_sums(True, BF16, "out_other"), "chan", partners)
    kept = out_sums(False, F32, "out_own")
    pair = (kept + given.astype(F32)).astype(BF16)
    terms = lax.all_to_all(pair, "chan", 0, 0, axis_index_groups=same_core, tiled=True)
    outgoing = kernel(refold_kernel, "refold", array((8 * SEQ, 128)), 8, 1 << 27, 9 * moved)(terms)
    returned = lax.all_to_all(outgoing.reshape(SEQ, 8, 128), "seq", 0, 0, tiled=True)
    return kernel(unpack_kernel, "unpack", array((rows, chans)), 4, 1 << 27, 2 * moved)(
        returned.reshape(8 * SEQ, 128)
    )


def solution(mesh):
    return jax.shard_map(
        body,
        mesh=mesh,
        in_specs=(
            P("seq", "chan"),
            P(None, None, "chan"),
            P(None, None, "chan"),
            P("chan", None),
            P("chan"),
            P("chan", None),
            P(),
        ),
        out_specs=P("seq", "chan"),
        check_vma=False,
    )
```

time: 193 us -> 165 us (0.85)
  Pallas kernels: 34.9 us -> 10.7 us
  waiting for transfers between devices: 0.13 us -> 3.26 us
  local copies, waits for them, and re-layouts: 3.37 us -> 0.94 us
  other arithmetic: 2.42 us -> 0.3 us
  blocking collectives: 136 us -> 134 us
    pallas_call x8 -> x10, Pallas kernels: 34.9 us -> 10.7 us  [call(): pl.pallas_call(body, out_shape=out_shape, in_specs=[anywhere if i in in_p...]
  transfers between devices with their start and end apart: 3 -> 3, of which waited for: 1 -> 2; matrix products, arithmetic and copies ran while one was open for 0% -> 0% of each run, Pallas kernels for 7% -> 2%
where the time goes in v2:
time: 165 us; the launch traced here: 163 us
  blocking collectives  134 us (81%)
  starting transfers between devices  13.4 us (8%)
  Pallas kernels  10.7 us (6%)
  waiting for transfers between devices  3.26 us (2%)
    all_to_all x1, blocking collectives, body(): lax.all_to_all(packed.reshape(SEQ, 8, 128), 'seq', 0, 0, tiled=True)  62.4 us
    all_to_all x1, blocking collectives, body(): lax.all_to_all(outgoing.reshape(SEQ, 8, 128), 'seq', 0, 0, tiled=True)  37.9 us
    all_to_all x1, blocking collectives, body(): lax.all_to_all(pair, 'chan', 0, 0, axis_index_groups=same_core, tiled=True)  18.3 us
    all_to_all x1, blocking collectives, body(): lax.all_to_all(spread, 'chan', 0, 0, axis_index_groups=same_core, tiled=T...  15.7 us
    pallas_call x10, Pallas kernels, call(): pl.pallas_call(body, out_shape=out_shape, in_specs=[anywhere if i in in_p...  10.7 us
    ppermute x1, starting transfers between devices, body(): far = lax.ppermute(near, 'chan', partners)  6.8 us
    ppermute x1, starting transfers between devices, body(): before = lax.ppermute(halo, 'seq', ahead)  3.79 us
  transfers between devices with their start and end apart: 3, of which 2 were waited for; matrix products, arithmetic and copies ran while one was open for 0% of the time, Pallas kernels for 2%

profile of v2, /device:TPU:1, one launch (start us, length us, event | category | flops | bytes accessed | tf_op | source)
XLA Modules:
  0.0 163.0 jit_solution(5004050116197408382)
XLA Ops:
  0.0 0.9 copy-done.1
  0.9 0.3 pack.1
  1.2 62.4 %all_to_all.20 = bf16[64,8,128]{2,1,0:T(8,128)(2,1)S(1)} all-to-all(bf16[64,8,128]{2,1,0:T(8,128)(2,1)S(1)} %bitcast.11), channel_id=1, replica_groups=mesh['seq'=64,'chan'=16] {'seq'}, dimensions={0} | all-to-all | bytes 262144 | tf_op jit(solution)/shard_map/all_to_all | solution.py:243
  63.6 0.3 unfold.1
  63.9 15.7 %all_to_all.21.rows = bf16[8,256,256]{2,1,0:T(8,128)(2,1)S(1)} all-to-all(bf16[8,256,256]{2,1,0:T(8,128)(2,1)S(1)} %unfold.1), channel_id=1, replica_groups={{0,2,4,6,8,10,12,14},{1,3,5,7,9,11,13,15},{16,18,20,22,24,26,28,30},{17..., dimensions={0} | all-to-all | bytes 2097152 | tf_op jit(solution)/shard_map/all_to_all | solution.py:247
  79.6 6.8 %collective-permute-start = (bf16[8,256,256]{2,1,0:T(8,128)(2,1)S(1)}, bf16[8,256,256]{2,1,0:T(8,128)(2,1)S(1)}, u32[]{:S(2)}, u32[]{:S(2)}) collective-permute-start(bf16[8,256,256]{2,1,0:T(8,128)(2,1)S(1)} %all_to_all.21.rows), channel_id=1, source_target_pairs={{0,1},{1,0},{2,3},{3,2},{4,5},{5,4},{6,7},{7,6},{8,9},{9,8},{10,11... | collective-permute-start | bytes 3145736 | tf_op jit(solution)/shard_map/ppermute | solution.py:248
  86.4 0.0 copy-start.2
  86.4 0.0 copy-start.3
  86.5 3.1 %project_near.1.partial = f32[3,256,256]{2,1,0:T(8,128)S(1)} custom-call(bf16[8,256,256]{2,1,0:T(8,128)(2,1)S(1)} %all_to_all.21.rows, bf16[3,8,2,256,256]{4,3,2,1,0:T(8,128)(2,1)} %bitcast.16), custom_call_target="tpu_custom_call" | custom-call | flops 805306368 | bytes 5242880 | tf_op jit(solution)/shard_map/project_near/pallas_call | solution.py:211
  89.6 0.0 copy-start.5
  89.6 3.1 %project_far.1 = (bf16[3,256,256]{2,1,0:T(8,128)(2,1)S(1)}, bf16[176,256]{1,0:T(8,128)(2,1)S(1)}) custom-call(bf16[8,256,256]{2,1,0:T(8,128)(2,1)S(1)} %collective-permute-done.rows, bf16[3,8,2,256,256]{4,3,2,1,0:T(8,128)(2,1)} %bitcast.17, f32[3,256,256]{2,1,0:T(8,128)S(1)} %project_near.1.partial, s32[128,128]{1,0:T(8,128)S(1)} %bitcast.13, ...), custom_call_target="tpu_custom_call" | custom-call | flops 805306368 | bytes 5242880 | tf_op jit(solution)/shard_map/project_far/pallas_call | solution.py:211
  92.8 3.8 %collective-permute-start.1 = (bf16[176,256]{1,0:T(8,128)(2,1)S(1)}, bf16[176,256]{1,0:T(8,128)(2,1)S(1)}, u32[]{:S(2)}, u32[]{:S(2)}) collective-permute-start(bf16[176,256]{1,0:T(8,128)(2,1)S(1)} %get-tuple-element.8), channel_id=1, source_target_pairs={{0,32},{32,64},{64,96},{96,128},{128,160},{160,192},{192,224},{224... | collective-permute-start | bytes 270344 | tf_op jit(solution)/shard_map/ppermute | solution.py:267
  96.6 0.5 bands.1
  97.0 1.5 collective-permute-done.1.halo
  98.5 1.1 mix.1.rows
  99.6 0.5 out_other.1
  100.1 2.8 %collective-permute-start.2 = (bf16[8,256,256]{2,1,0:T(8,128)(2,1)S(1)}, bf16[8,256,256]{2,1,0:T(8,128)(2,1)S(1)}, u32[]{:S(2)}, u32[]{:S(2)}) collective-permute-start(bf16[8,256,256]{2,1,0:T(8,128)(2,1)S(1)} %out_other.1), channel_id=1, source_target_pairs={{0,1},{1,0},{2,3},{3,2},{4,5},{5,4},{6,7},{7,6},{8,9},{9,8},{10,11... | collective-permute-start | bytes 3145736 | tf_op jit(solution)/shard_map/ppermute | solution.py:282
  102.9 0.5 out_own.1
  103.3 1.8 %collective-permute-done.2 = bf16[8,256,256]{2,1,0:T(8,128)(2,1)S(1)} collective-permute-done((bf16[8,256,256]{2,1,0:T(8,128)(2,1)S(1)}, bf16[8,256,256]{2,1,0:T(8,128)(2,1)S(1)}, u32[]{:S(2)}, u32[]{:S(2)}) %collective-permute-start.2) | collective-permute-done | bytes 1048608 | tf_op jit(solution)/shard_map/ppermute | solution.py:282
  105.1 0.3 add_convert_fusion
  105.4 18.3 %all_to_all.22.terms = bf16[8,256,256]{2,1,0:T(8,128)(2,1)S(1)} all-to-all(bf16[8,256,256]{2,1,0:T(8,128)(2,1)S(1)} %add_convert_fusion), channel_id=1, replica_groups={{0,2,4,6,8,10,12,14},{1,3,5,7,9,11,13,15},{16,18,20,22,24,26,28,30},{17..., dimensions={0} | all-to-all | bytes 2097152 | tf_op jit(solution)/shard_map/all_to_all | solution.py:285
  123.7 0.4 refold.1
  124.1 37.9 %all_to_all.23 = bf16[64,8,128]{2,1,0:T(8,128)(2,1)S(1)} all-to-all(bf16[64,8,128]{2,1,0:T(8,128)(2,1)S(1)} %bitcast.10), channel_id=1, replica_groups=mesh['seq'=64,'chan'=16] {'seq'}, dimensions={0} | all-to-all | bytes 262144 | tf_op jit(solution)/shard_map/all_to_all | solution.py:287
  162.0 1.0 unpack.1
  (9 shorter events, 0.0 us)
Async XLA Ops:
  0.0 0.9 copy-start.1
  79.6 9.9 %collective-permute-start = (bf16[8,256,256]{2,1,0:T(8,128)(2,1)S(1)}, bf16[8,256,256]{2,1,0:T(8,128)(2,1)S(1)}, u32[]{:S(2)}, u32[]{:S(2)}) collective-permute-start(bf16[8,256,256]{2,1,0:T(8,128)(2,1)S(1)} %all_to_all.21.rows), channel_id=1, source_target_pairs={{0,1},{1,0},{2,3},{3,2},{4,5},{5,4},{6,7},{7,6},{8,9},{9,8},{10,11... | collective-permute-start | bytes 3145736 | tf_op jit(solution)/shard_map/ppermute | solution.py:248
  86.4 3.1 %copy-start.2 = (s32[16384]{0:T(1024)S(1)}, s32[16384]{0:T(1024)}, u32[]{:S(2)}) copy-start(s32[16384]{0:T(1024)} %param.13) | copy-start | bytes 196612
  86.4 3.1 %copy-start.3 = (f32[3,3,256]{2,1,0:T(4,128)S(1)}, f32[3,3,256]{2,1,0:T(4,128)}, u32[]{:S(2)}) copy-start(f32[3,3,256]{2,1,0:T(4,128)} %short_filter.3) | copy-start | bytes 27652
  89.6 7.0 %copy-start.4 = (bf16[16,128]{1,0:T(8,128)(2,1)S(1)}, bf16[16,128]{1,0:T(8,128)(2,1)}, u32[]{:S(2)}) copy-start(bf16[16,128]{1,0:T(8,128)(2,1)} %filters.1) | copy-start | bytes 12292
  89.6 8.9 %copy-start.5 = (f32[256]{0:T(256)S(1)}, f32[256]{0:T(256)}, u32[]{:S(2)}) copy-start(f32[256]{0:T(256)} %param.11) | copy-start | bytes 3076
  92.8 6.9 %copy-start = (bf16[256,4096]{1,0:T(8,128)(2,1)S(1)}, bf16[256,4096]{1,0:T(8,128)(2,1)}, u32[]{:S(2)}) copy-start(bf16[256,4096]{1,0:T(8,128)(2,1)} %weights.3) | copy-start | bytes 6291460
  92.8 5.7 %collective-permute-start.1 = (bf16[176,256]{1,0:T(8,128)(2,1)S(1)}, bf16[176,256]{1,0:T(8,128)(2,1)S(1)}, u32[]{:S(2)}, u32[]{:S(2)}) collective-permute-start(bf16[176,256]{1,0:T(8,128)(2,1)S(1)} %get-tuple-element.8), channel_id=1, source_target_pairs={{0,32},{32,64},{64,96},{96,128},{128,160},{160,192},{192,224},{224... | collective-permute-start | bytes 270344 | tf_op jit(solution)/shard_map/ppermute | solution.py:267
  100.1 5.0 %collective-permute-start.2 = (bf16[8,256,256]{2,1,0:T(8,128)(2,1)S(1)}, bf16[8,256,256]{2,1,0:T(8,128)(2,1)S(1)}, u32[]{:S(2)}, u32[]{:S(2)}) collective-permute-start(bf16[8,256,256]{2,1,0:T(8,128)(2,1)S(1)} %out_other.1), channel_id=1, source_target_pairs={{0,1},{1,0},{2,3},{3,2},{4,5},{5,4},{6,7},{7,6},{8,9},{9,8},{10,11... | collective-permute-start | bytes 3145736 | tf_op jit(solution)/shard_map/ppermute | solution.py:282

commit v3 on v2

--- a/solution.py
+++ b/solution.py
@@ -1,5 +1,3 @@
-import functools
-
 import jax
 import jax.numpy as jnp
 from jax import lax
@@ -51,13 +49,15 @@
     packed[...] = moved.astype(BF16)
 
 
-def unpack_kernel(packed, rows):
-    shape = (rows.shape[0], packed.shape[0])
+def unpack(packed, count):
+    shape = (count, packed.shape[0])
     target, source = iota(shape, 0), iota(shape, 1)
+    mine = block_of(source // 8) == target // 4
+    halves = []
     for part in range(2):
-        wanted = (block_of(source // 8) == target // 4) & (source % 8 == 4 * part + target % 4)
-        moved = dot(wanted.astype(BF16), packed[...])
-        rows[:, 128 * part : 128 * (part + 1)] = moved.astype(BF16)
+        pick = mine & (source % 8 == 4 * part + target % 4)
+        halves.append(dot(pick.astype(BF16), packed[...]).astype(BF16))
+    return jnp.concatenate(halves, axis=1)
 
 
 def unfold_kernel(received, spread):
@@ -72,20 +72,23 @@
             spread[copy, :, 128 * part : 128 * (part + 1)] = moved
 
 
-def refold_kernel(terms, outgoing):
-    total = terms[0].astype(F32)
-    for term in range(1, terms.shape[0]):
-        total = total + terms[term].astype(F32)
-    mixed = total.astype(BF16)
-    shape = (outgoing.shape[0], mixed.shape[0])
+def refold(gated, outgoing):
+    shape = (outgoing.shape[0], gated.shape[0])
     device, slot = fold_source(iota(shape, 1))
     target = iota(shape, 0)
     moved = None
     for part in range(2):
         pick = (target == device * 8 + part * 4 + slot).astype(BF16)
-        term = dot(pick, mixed[:, 128 * part : 128 * (part + 1)])
+        term = dot(pick, gated[:, 128 * part : 128 * (part + 1)])
         moved = term if moved is None else moved + term
     outgoing[...] = moved.astype(BF16)
+
+
+def sum_kernel(terms, mixed):
+    total = terms[0].astype(F32)
+    for term in range(1, terms.shape[0]):
+        total = total + terms[term].astype(F32)
+    mixed[...] = total.astype(BF16)
 
 
 def segment_columns(segments, first, count):
@@ -106,38 +109,35 @@
     return result
 
 
-def project(other, rows, weights, fetched, sems, finish):
+def join(blocks):
+    return jnp.concatenate([blocks[chip] for chip in range(blocks.shape[0])], axis=1)
+
+
+def project_near_kernel(rows, weights, partial, far_lines, lines, sems):
+    core = lax.axis_index("chan") % 2
     chips, _, width = rows.shape
-    core = lax.axis_index("chan") % 2
-    parity = 1 - core if other else core
     copies = [
-        pltpu.make_async_copy(weights.at[part, :, parity], fetched.at[part], sems.at[part])
+        pltpu.make_async_copy(weights.at[part, :, core], lines.at[part], sems.at[part])
         for part in range(3)
     ]
+    copies.append(pltpu.make_async_copy(weights.at[:, :, 1 - core], far_lines, sems.at[3]))
     for copy in copies:
         copy.start()
-    data = jnp.concatenate([rows[chip] for chip in range(chips)], axis=1)
+    data = join(rows)
     for part in range(3):
         copies[part].wait()
-        finish(part, dot(data, fetched[part].reshape(chips * width, width)))
-
-
-def project_near_kernel(rows, weights, partial, fetched, sems):
-    def finish(part, total):
-        partial[part] = total
-
-    project(False, rows, weights, fetched, sems, finish)
-
-
-def project_far_kernel(rows, weights, partial, segments, short_filter, qkv, halo, fetched, sems):
-    count = qkv.shape[1]
-
-    def finish(part, total):
-        rounded = (partial[part] + total).astype(BF16)
+        partial[part] = dot(data, lines[part].reshape(chips * width, width))
+    copies[3].wait()
+
+
+def project_far_kernel(rows, lines, partial, segments, short_filter, qkv, halo):
+    chips, count, width = rows.shape
+    data = join(rows)
+    for part in range(3):
+        total = partial[part] + dot(data, lines[part].reshape(chips * width, width))
+        rounded = total.astype(BF16)
         qkv[part] = rounded
         halo[128 + 16 * part : 144 + 16 * part, :] = rounded[count - 16 :]
-
-    project(True, rows, weights, fetched, sems, finish)
     block = block_of(lax.axis_index("seq"))
     columns = segment_columns(segments, 2 * block, 2)[count - 136 :]
     pair = []
@@ -157,7 +157,7 @@
         bands[group] = pltpu.roll(row, 0, 1, stride=1, stride_axis=0).astype(BF16)
 
 
-def mix_kernel(qkv, halo, bands, segments, short_filter, skip_gain, gated_out):
+def mix_kernel(qkv, halo, bands, segments, short_filter, skip_gain, outgoing, gated_out):
     seq = block_of(lax.axis_index("seq"))
     count, chans = gated_out.shape
     groups = bands.shape[0]
@@ -192,15 +192,33 @@
             rows = slice(128 * block, 128 * (block + 1))
             direct = skip_gain[:, lanes] * gated[rows, lanes].astype(F32)
             gated_out[rows, lanes] = (convolved[0][rows, lanes] * (total + direct)).astype(BF16)
-
-
-def out_kernel(other, rows, weights, sums):
+    refold(gated_out, outgoing)
+
+
+def pick_kernel(weights, given, kept, sems):
     core = lax.axis_index("chan") % 2
-    parity = 1 - core if other else core
-    chips, _, width = sums.shape
-    for chip in range(chips):
-        columns = pl.ds(pl.multiple_of((2 * chip + parity) * width, width), width)
-        sums[chip] = dot(rows[...], weights[:, columns]).astype(sums.dtype)
+    copies = []
+    for i, (lines, parity) in enumerate(((given, 1 - core), (kept, core))):
+        chips, _, width = lines.shape
+        for chip in range(chips):
+            columns = pl.ds(pl.multiple_of((2 * chip + parity) * width, width), width)
+            copies.append(pltpu.make_async_copy(weights.at[:, columns], lines.at[chip], sems.at[i, chip]))
+    for copy in copies:
+        copy.start()
+    for copy in copies:
+        copy.wait()
+
+
+def out_near_kernel(packed, lines, sums):
+    rows = unpack(packed, sums.shape[1])
+    for chip in range(sums.shape[0]):
+        sums[chip] = dot(rows, lines[chip])
+
+
+def out_far_kernel(packed, lines, near, sums):
+    rows = unpack(packed, sums.shape[1])
+    for chip in range(sums.shape[0]):
+        sums[chip] = (near[chip] + dot(rows, lines[chip])).astype(BF16)
 
 
 def kernel(body, name, out_shape, mib, flops, moved, in_place=(), scratch=()):
@@ -224,6 +242,11 @@
 
 def array(shape, dtype=BF16):
     return jax.ShapeDtypeStruct(shape, dtype)
+
+
+def over_seq(packed):
+    chunks = packed.reshape(SEQ, 8, 128)
+    return lax.all_to_all(chunks, "seq", 0, 0, tiled=True).reshape(8 * SEQ, 128)
 
 
 def body(tokens, w_in, short_filter, mr_filter, skip_gain, w_out, segments):
@@ -240,54 +263,47 @@
     moved = rows * chans * 2
 
     packed = kernel(pack_kernel, "pack", array((8 * SEQ, 128)), 4, 1 << 26, 2 * moved)(tokens)
-    received = lax.all_to_all(packed.reshape(SEQ, 8, 128), "seq", 0, 0, tiled=True)
-    spread = kernel(unfold_kernel, "unfold", array((chips, rows, chans)), 8, 1 << 27, 9 * moved)(
-        received.reshape(8 * SEQ, 128)
-    )
+    spread = kernel(unfold_kernel, "unfold", array((chips, rows, chans)), 8, 1 << 27, 9 * moved)(over_seq(packed))
     near = lax.all_to_all(spread, "chan", 0, 0, axis_index_groups=same_core, tiled=True)
     far = lax.ppermute(near, "chan", partners)
     bands = kernel(band_kernel, "bands", array((mr_filter.shape[0], 128, 256)), 8, 1 << 24, 8 * moved)(mr_filter)
     weights = w_in.transpose(1, 0, 2).reshape(3, chips, 2, chans, chans)
+    lines = (3, chips, chans, chans)
     work = 3 * rows * width * chans
-    scratch = [pltpu.VMEM((3, chips, chans, chans), BF16), pltpu.SemaphoreType.DMA((3,))]
-    partial = kernel(
-        project_near_kernel, "project_near", array((3, rows, chans), F32), 51, work, 40 * moved, (1,), scratch
+    partial, far_lines = kernel(
+        project_near_kernel,
+        "project_near",
+        (array((3, rows, chans), F32), array(lines)),
+        47,
+        work,
+        60 * moved,
+        (1,),
+        [pltpu.VMEM(lines, BF16), pltpu.SemaphoreType.DMA((4,))],
     )(near, weights)
     qkv, halo = kernel(
         project_far_kernel,
         "project_far",
         (array((3, rows, chans)), array((176, chans))),
-        51,
+        8,
         work,
         40 * moved,
-        (1,),
-        scratch,
-    )(far, weights, partial, segments, short_filter)
+    )(far, far_lines, partial, segments, short_filter)
 
     before = lax.ppermute(halo, "seq", ahead)
-    gated_out = kernel(mix_kernel, "mix", array((rows, chans)), 8, 1 << 29, 16 * moved)(
-        qkv, before, bands, segments, short_filter, gain
-    )
-
-    def out_sums(other, dtype, name):
-        return kernel(
-            functools.partial(out_kernel, other),
-            name,
-            array((chips, rows, chans), dtype),
-            8,
-            rows * width * chans,
-            16 * moved,
-        )(gated_out, w_out)
-
-    given = lax.ppermute(out_sums(True, BF16, "out_other"), "chan", partners)
-    kept = out_sums(False, F32, "out_own")
-    pair = (kept + given.astype(F32)).astype(BF16)
-    terms = lax.all_to_all(pair, "chan", 0, 0, axis_index_groups=same_core, tiled=True)
-    outgoing = kernel(refold_kernel, "refold", array((8 * SEQ, 128)), 8, 1 << 27, 9 * moved)(terms)
-    returned = lax.all_to_all(outgoing.reshape(SEQ, 8, 128), "seq", 0, 0, tiled=True)
-    return kernel(unpack_kernel, "unpack", array((rows, chans)), 4, 1 << 27, 2 * moved)(
-        returned.reshape(8 * SEQ, 128)
-    )
+    block = array((chips, rows, chans))
+    given, kept = kernel(
+        pick_kernel, "pick", (block, block), 8, 0, 32 * moved, (0,), [pltpu.SemaphoreType.DMA((2, chips))]
+    )(w_out)
+    taken = lax.ppermute(given, "chan", partners)
+    outgoing = kernel(
+        mix_kernel, "mix", array((8 * SEQ, 128)), 8, 1 << 29, 16 * moved, (), [pltpu.VMEM((rows, chans), BF16)]
+    )(qkv, before, bands, segments, short_filter, gain)
+    returned = over_seq(outgoing)
+    other = lax.ppermute(returned, "chan", partners)
+    sums = kernel(out_near_kernel, "out_near", array(block.shape, F32), 8, work // 3, 16 * moved)(returned, kept)
+    sums = kernel(out_far_kernel, "out_far", block, 8, work // 3, 16 * moved)(other, taken, sums)
+    terms = lax.all_to_all(sums, "chan", 0, 0, axis_index_groups=same_core, tiled=True)
+    return kernel(sum_kernel, "sum", array((rows, chans)), 4, 1 << 20, 9 * moved)(terms)
 
 
 def solution(mesh):

time: 165 us -> 164 us (level)
  blocking collectives: 134 us -> 96.3 us
  waiting for transfers between devices: 3.26 us -> 26.8 us
  starting transfers between devices: 13.4 us -> 28 us
    all_to_all x3 -> x2, blocking collectives: 119 us -> 80.6 us  [the longest x1 62.4 us: over_seq(): return lax.all_to_all(chunks, 'seq', 0, 0, tiled=True).reshape(8 * SEQ, 128)]
    all_to_all x0 -> x1, waiting for transfers between devices: none -> 25 us  [over_seq(): return lax.all_to_all(chunks, 'seq', 0, 0, tiled=True).reshape(8 * SEQ, 128)]
    all_to_all x0 -> x1, starting transfers between devices: none -> 8.31 us  [over_seq(): return lax.all_to_all(chunks, 'seq', 0, 0, tiled=True).reshape(8 * SEQ, 128)]
    ppermute x1 -> x2, starting transfers between devices: 2.78 us -> 9.26 us  [the longest x1 6.2 us: body(): other = lax.ppermute(returned, 'chan', partners)]
  transfers between devices with their start and end apart: 3 -> 5, of which waited for: 2 -> 3; matrix products, arithmetic and copies ran while one was open for 0% -> 0% of each run, Pallas kernels for 2% -> 4%
where the time goes in v3:
time: 164 us; the launch traced here: 163 us
  blocking collectives  96.3 us (59%)
  starting transfers between devices  28 us (17%)
  waiting for transfers between devices  26.8 us (16%)
  Pallas kernels  10.9 us (7%)
    all_to_all x1, blocking collectives, over_seq(): return lax.all_to_all(chunks, 'seq', 0, 0, tiled=True).reshape(8 * SEQ, 128)  62.4 us
    all_to_all x1, waiting for transfers between devices, over_seq(): return lax.all_to_all(chunks, 'seq', 0, 0, tiled=True).reshape(8 * SEQ, 128)  25 us
    all_to_all x1, blocking collectives, body(): lax.all_to_all(sums, 'chan', 0, 0, axis_index_groups=same_core, tiled=True)  18.3 us
    all_to_all x1, blocking collectives, body(): lax.all_to_all(spread, 'chan', 0, 0, axis_index_groups=same_core, tiled=T...  15.7 us
    pallas_call x10, Pallas kernels, call(): pl.pallas_call(body, out_shape=out_shape, in_specs=[anywhere if i in in_p...  10.9 us
    all_to_all x1, starting transfers between devices, over_seq(): return lax.all_to_all(chunks, 'seq', 0, 0, tiled=True).reshape(8 * SEQ, 128)  8.31 us
    ppermute x1, starting transfers between devices, body(): far = lax.ppermute(near, 'chan', partners)  6.8 us
    ppermute x1, starting transfers between devices, body(): other = lax.ppermute(returned, 'chan', partners)  6.2 us
  transfers between devices with their start and end apart: 5, of which 3 were waited for; matrix products, arithmetic and copies ran while one was open for 0% of the time, Pallas kernels for 4%

profile of v3, /device:TPU:1, one launch (start us, length us, event | category | flops | bytes accessed | tf_op | source)
XLA Modules:
  0.0 163.2 jit_solution(9616164469348145464)
XLA Ops:
  0.0 0.9 copy-done.1
  0.9 0.3 pack.1
  1.2 62.4 %all_to_all.20 = bf16[64,8,128]{2,1,0:T(8,128)(2,1)S(1)} all-to-all(bf16[64,8,128]{2,1,0:T(8,128)(2,1)S(1)} %bitcast.12), channel_id=1, replica_groups=mesh['seq'=64,'chan'=16] {'seq'}, dimensions={0} | all-to-all | bytes 262144 | tf_op jit(solution)/shard_map/all_to_all | solution.py:249
  63.6 0.3 unfold.1
  63.9 15.7 %all_to_all.21.rows = bf16[8,256,256]{2,1,0:T(8,128)(2,1)S(1)} all-to-all(bf16[8,256,256]{2,1,0:T(8,128)(2,1)S(1)} %unfold.1), channel_id=1, replica_groups={{0,2,4,6,8,10,12,14},{1,3,5,7,9,11,13,15},{16,18,20,22,24,26,28,30},{17..., dimensions={0} | all-to-all | bytes 2097152 | tf_op jit(solution)/shard_map/all_to_all | solution.py:267
  79.6 6.8 %collective-permute-start = (bf16[8,256,256]{2,1,0:T(8,128)(2,1)S(1)}, bf16[8,256,256]{2,1,0:T(8,128)(2,1)S(1)}, u32[]{:S(2)}, u32[]{:S(2)}) collective-permute-start(bf16[8,256,256]{2,1,0:T(8,128)(2,1)S(1)} %all_to_all.21.rows), channel_id=1, source_target_pairs={{0,1},{1,0},{2,3},{3,2},{4,5},{5,4},{6,7},{7,6},{8,9},{9,8},{10,11... | collective-permute-start | bytes 3145736 | tf_op jit(solution)/shard_map/ppermute | solution.py:268
  86.4 0.0 copy-start.3
  86.5 3.1 %project_near.1 = (f32[3,256,256]{2,1,0:T(8,128)S(1)}, bf16[3,8,256,256]{3,2,1,0:T(8,128)(2,1)S(1)}) custom-call(bf16[8,256,256]{2,1,0:T(8,128)(2,1)S(1)} %all_to_all.21.rows, bf16[3,8,2,256,256]{4,3,2,1,0:T(8,128)(2,1)} %bitcast.16), custom_call_target="tpu_custom_call" | custom-call | flops 805306368 | bytes 7864320 | tf_op jit(solution)/shard_map/project_near/pallas_call | solution.py:229
  89.6 0.0 copy-start.5
  89.6 1.1 project_far.1
  90.7 3.7 %collective-permute-start.1 = (bf16[176,256]{1,0:T(8,128)(2,1)S(1)}, bf16[176,256]{1,0:T(8,128)(2,1)S(1)}, u32[]{:S(2)}, u32[]{:S(2)}) collective-permute-start(bf16[176,256]{1,0:T(8,128)(2,1)S(1)} %get-tuple-element.14), channel_id=1, source_target_pairs={{0,32},{32,64},{64,96},{96,128},{128,160},{160,192},{192,224},{224... | collective-permute-start | bytes 270344 | tf_op jit(solution)/shard_map/ppermute | solution.py:292
  94.4 0.5 bands.1
  94.9 1.5 collective-permute-done.1.halo
  96.3 2.0 %mix.1 = bf16[512,128]{1,0:T(8,128)(2,1)} custom-call(bf16[3,256,256]{2,1,0:T(8,128)(2,1)S(1)} %get-tuple-element.13.qkv, bf16[176,256]{1,0:T(8,128)(2,1)S(1)} %collective-permute-done.1.halo, bf16[16,128,256]{2,1,0:T(8,128)(2,1)S(1)} %bands.1, s32[128,128]{1,0:T(8,128)S(1)} %bitcast.14, f32[3,3,256]{2,1,0:T(4,128)S(1)} %copy-done.3, f32[1,256]{1,0:T(1,128)S(1)} %bitcast.15), custom_call_target="tpu_custom_call" | custom-call | flops 536870912 | bytes 2097152 | tf_op jit(solution)/shard_map/mix/pallas_call | solution.py:229
  98.4 8.3 %all-to-all-start.2 = ((bf16[64,8,128]{2,1,0:T(8,128)(2,1)}), bf16[64,8,128]{2,1,0:T(8,128)(2,1)S(1)}, u32[]{:S(2)}, u32[]{:S(2)}) async-start(bf16[64,8,128]{2,1,0:T(8,128)(2,1)} %bitcast.6), calls=%async_computation.2 | async-start | bytes 262144 | tf_op jit(solution)/shard_map/all_to_all | solution.py:249
  106.7 1.5 pick.1
  108.2 3.1 %collective-permute-start.3 = (bf16[8,256,256]{2,1,0:T(8,128)(2,1)}, bf16[8,256,256]{2,1,0:T(8,128)(2,1)S(1)}, u32[]{:S(2)}, u32[]{:S(2)}) collective-permute-start(bf16[8,256,256]{2,1,0:T(8,128)(2,1)} %get-tuple-element.15), channel_id=1, source_target_pairs={{0,1},{1,0},{2,3},{3,2},{4,5},{5,4},{6,7},{7,6},{8,9},{9,8},{10,11... | collective-permute-start | bytes 3145736 | tf_op jit(solution)/shard_map/ppermute | solution.py:297
  111.3 25.0 %all-to-all-done.2 = bf16[64,8,128]{2,1,0:T(8,128)(2,1)S(1)} async-done(((bf16[64,8,128]{2,1,0:T(8,128)(2,1)}), bf16[64,8,128]{2,1,0:T(8,128)(2,1)S(1)}, u32[]{:S(2)}, u32[]{:S(2)}) %all-to-all-start.2) | async-done | bytes 131104 | tf_op jit(solution)/shard_map/all_to_all | solution.py:249
  136.3 6.2 %collective-permute-start.2 = (bf16[512,128]{1,0:T(8,128)(2,1)S(1)}, bf16[512,128]{1,0:T(8,128)(2,1)S(1)}, u32[]{:S(2)}, u32[]{:S(2)}) collective-permute-start(bf16[512,128]{1,0:T(8,128)(2,1)S(1)} %bitcast.9), channel_id=1, source_target_pairs={{0,1},{1,0},{2,3},{3,2},{4,5},{5,4},{6,7},{7,6},{8,9},{9,8},{10,11... | collective-permute-start | bytes 393224 | tf_op jit(solution)/shard_map/ppermute | solution.py:302
  142.5 0.7 out_near.1.near
  143.2 0.3 collective-permute-done.2.packed
  143.4 0.7 out_far.1
  144.1 18.3 %all_to_all.22.terms = bf16[8,256,256]{2,1,0:T(8,128)(2,1)S(1)} all-to-all(bf16[8,256,256]{2,1,0:T(8,128)(2,1)S(1)} %out_far.1), channel_id=1, replica_groups={{0,2,4,6,8,10,12,14},{1,3,5,7,9,11,13,15},{16,18,20,22,24,26,28,30},{17..., dimensions={0} | all-to-all | bytes 2097152 | tf_op jit(solution)/shard_map/all_to_all | solution.py:305
  162.4 0.8 sum.1
  (11 shorter events, 0.0 us)
Async XLA Ops:
  0.0 0.9 copy-start.1
  79.6 10.0 %collective-permute-start = (bf16[8,256,256]{2,1,0:T(8,128)(2,1)S(1)}, bf16[8,256,256]{2,1,0:T(8,128)(2,1)S(1)}, u32[]{:S(2)}, u32[]{:S(2)}) collective-permute-start(bf16[8,256,256]{2,1,0:T(8,128)(2,1)S(1)} %all_to_all.21.rows), channel_id=1, source_target_pairs={{0,1},{1,0},{2,3},{3,2},{4,5},{5,4},{6,7},{7,6},{8,9},{9,8},{10,11... | collective-permute-start | bytes 3145736 | tf_op jit(solution)/shard_map/ppermute | solution.py:268
  86.4 3.2 %copy-start.2 = (s32[16384]{0:T(1024)S(1)}, s32[16384]{0:T(1024)}, u32[]{:S(2)}) copy-start(s32[16384]{0:T(1024)} %param.13) | copy-start | bytes 196612
  86.4 3.2 %copy-start.3 = (f32[3,3,256]{2,1,0:T(4,128)S(1)}, f32[3,3,256]{2,1,0:T(4,128)}, u32[]{:S(2)}) copy-start(f32[3,3,256]{2,1,0:T(4,128)} %short_filter.3) | copy-start | bytes 27652
  89.6 4.8 %copy-start.4 = (bf16[16,128]{1,0:T(8,128)(2,1)S(1)}, bf16[16,128]{1,0:T(8,128)(2,1)}, u32[]{:S(2)}) copy-start(bf16[16,128]{1,0:T(8,128)(2,1)} %filters.1) | copy-start | bytes 12292
  89.6 6.8 %copy-start.5 = (f32[256]{0:T(256)S(1)}, f32[256]{0:T(256)}, u32[]{:S(2)}) copy-start(f32[256]{0:T(256)} %param.11) | copy-start | bytes 3076
  89.6 17.1 %copy-start = (bf16[256,4096]{1,0:T(8,128)(2,1)S(1)}, bf16[256,4096]{1,0:T(8,128)(2,1)}, u32[]{:S(2)}) copy-start(bf16[256,4096]{1,0:T(8,128)(2,1)} %weights.1) | copy-start | bytes 6291460
  90.7 5.6 %collective-permute-start.1 = (bf16[176,256]{1,0:T(8,128)(2,1)S(1)}, bf16[176,256]{1,0:T(8,128)(2,1)S(1)}, u32[]{:S(2)}, u32[]{:S(2)}) collective-permute-start(bf16[176,256]{1,0:T(8,128)(2,1)S(1)} %get-tuple-element.14), channel_id=1, source_target_pairs={{0,32},{32,64},{64,96},{96,128},{128,160},{160,192},{192,224},{224... | collective-permute-start | bytes 270344 | tf_op jit(solution)/shard_map/ppermute | solution.py:292
  98.4 37.9 %all-to-all-start.2 = ((bf16[64,8,128]{2,1,0:T(8,128)(2,1)}), bf16[64,8,128]{2,1,0:T(8,128)(2,1)S(1)}, u32[]{:S(2)}, u32[]{:S(2)}) async-start(bf16[64,8,128]{2,1,0:T(8,128)(2,1)} %bitcast.6), calls=%async_computation.2 | async-start | bytes 262144 | tf_op jit(solution)/shard_map/all_to_all | solution.py:249
  108.2 35.0 %collective-permute-start.3 = (bf16[8,256,256]{2,1,0:T(8,128)(2,1)}, bf16[8,256,256]{2,1,0:T(8,128)(2,1)S(1)}, u32[]{:S(2)}, u32[]{:S(2)}) collective-permute-start(bf16[8,256,256]{2,1,0:T(8,128)(2,1)} %get-tuple-element.15), channel_id=1, source_target_pairs={{0,1},{1,0},{2,3},{3,2},{4,5},{5,4},{6,7},{7,6},{8,9},{9,8},{10,11... | collective-permute-start | bytes 3145736 | tf_op jit(solution)/shard_map/ppermute | solution.py:297
  136.3 7.2 %collective-permute-start.2 = (bf16[512,128]{1,0:T(8,128)(2,1)S(1)}, bf16[512,128]{1,0:T(8,128)(2,1)S(1)}, u32[]{:S(2)}, u32[]{:S(2)}) collective-permute-start(bf16[512,128]{1,0:T(8,128)(2,1)S(1)} %bitcast.9), channel_id=1, source_target_pairs={{0,1},{1,0},{2,3},{3,2},{4,5},{5,4},{6,7},{7,6},{8,9},{9,8},{10,11... | collective-permute-start | bytes 393224 | tf_op jit(solution)/shard_map/ppermute | solution.py:302

commit v4 on v3

--- a/solution.py
+++ b/solution.py
@@ -31,16 +31,21 @@
     return jnp.where(half == 0, z, SEQ - 1 - z)
 
 
+def peer(chunk):
+    return chunk ^ (SEQ // 2)
+
+
 def fold_source(position):
     period, phase = position // (2 * SEQ), position % (2 * SEQ)
     late = phase >= SEQ
-    return jnp.where(late, 2 * SEQ - 1 - phase, phase), 2 * period + late.astype(jnp.int32)
+    device = jnp.where(late, 2 * SEQ - 1 - phase, phase)
+    return peer(device), 2 * period + late.astype(jnp.int32)
 
 
 def pack_kernel(tokens, packed):
     shape = (packed.shape[0], tokens.shape[0])
     target, source = iota(shape, 0), iota(shape, 1)
-    wanted = 4 * block_of(target // 8) + target % 4
+    wanted = 4 * block_of(peer(target // 8)) + target % 4
     moved = None
     for part in range(2):
         pick = (source == wanted) & (target // 4 % 2 == part)
@@ -52,7 +57,7 @@
 def unpack(packed, count):
     shape = (count, packed.shape[0])
     target, source = iota(shape, 0), iota(shape, 1)
-    mine = block_of(source // 8) == target // 4
+    mine = block_of(peer(source // 8)) == target // 4
     halves = []
     for part in range(2):
         pick = mine & (source % 8 == 4 * part + target % 4)
@@ -246,7 +251,8 @@
 
 def over_seq(packed):
     chunks = packed.reshape(SEQ, 8, 128)
-    return lax.all_to_all(chunks, "seq", 0, 0, tiled=True).reshape(8 * SEQ, 128)
+    order = [[peer(chunk) for chunk in range(SEQ)]]
+    return lax.all_to_all(chunks, "seq", 0, 0, axis_index_groups=order, tiled=True).reshape(8 * SEQ, 128)
 
 
 def body(tokens, w_in, short_filter, mr_filter, skip_gain, w_out, segments):

time: 164 us -> 152 us (0.927)
  waiting for transfers between devices: 26.8 us -> 10.9 us
  starting transfers between devices: 28 us -> 38.4 us
  blocking collectives: 96.3 us -> 89.9 us
    all_to_all x1, starting transfers between devices: 8.31 us -> 25.3 us  [over_seq(): lax.all_to_all(chunks, 'seq', 0, 0, axis_index_groups=order, tiled=True)]
    all_to_all x1, waiting for transfers between devices: 25 us -> 9.2 us  [over_seq(): lax.all_to_all(chunks, 'seq', 0, 0, axis_index_groups=order, tiled=True)]
    all_to_all x1, blocking collectives: 62.4 us -> 53.1 us  [over_seq(): lax.all_to_all(chunks, 'seq', 0, 0, axis_index_groups=order, tiled=True)]
    ppermute x1, starting transfers between devices: 6.2 us -> 3.07 us  [body(): other = lax.ppermute(returned, 'chan', partners)]
    ppermute x1, starting transfers between devices: 6.8 us -> 3.99 us  [body(): far = lax.ppermute(near, 'chan', partners)]
    all_to_all x1, blocking collectives: 15.7 us -> 18.5 us  [body(): lax.all_to_all(spread, 'chan', 0, 0, axis_index_groups=same_core, tiled=T...]
where the time goes in v4:
time: 152 us; the launch traced here: 151 us
  blocking collectives  89.9 us (59%)
  starting transfers between devices  38.4 us (25%)
  Pallas kernels  11 us (7%)
  waiting for transfers between devices  10.9 us (7%)
    all_to_all x1, blocking collectives, over_seq(): lax.all_to_all(chunks, 'seq', 0, 0, axis_index_groups=order, tiled=True)  53.1 us
    all_to_all x1, starting transfers between devices, over_seq(): lax.all_to_all(chunks, 'seq', 0, 0, axis_index_groups=order, tiled=True)  25.3 us
    all_to_all x1, blocking collectives, body(): lax.all_to_all(spread, 'chan', 0, 0, axis_index_groups=same_core, tiled=T...  18.5 us
    all_to_all x1, blocking collectives, body(): lax.all_to_all(sums, 'chan', 0, 0, axis_index_groups=same_core, tiled=True)  18.3 us
    pallas_call x10, Pallas kernels, call(): pl.pallas_call(body, out_shape=out_shape, in_specs=[anywhere if i in in_p...  11 us
    all_to_all x1, waiting for transfers between devices, over_seq(): lax.all_to_all(chunks, 'seq', 0, 0, axis_index_groups=order, tiled=True)  9.2 us
    ppermute x1, starting transfers between devices, body(): far = lax.ppermute(near, 'chan', partners)  3.99 us
    ppermute x1, starting transfers between devices, body(): taken = lax.ppermute(given, 'chan', partners)  3.34 us
  transfers between devices with their start and end apart: 5, of which 3 were waited for; matrix products, arithmetic and copies ran while one was open for 0% of the time, Pallas kernels for 4%

profile of v4, /device:TPU:1, one launch (start us, length us, event | category | flops | bytes accessed | tf_op | source)
XLA Modules:
  0.0 151.3 jit_solution(15793295047834274873)
XLA Ops:
  0.0 0.9 copy-done.1
  0.9 0.4 pack.1
  1.3 53.1 %all_to_all.20 = bf16[64,8,128]{2,1,0:T(8,128)(2,1)S(1)} all-to-all(bf16[64,8,128]{2,1,0:T(8,128)(2,1)S(1)} %bitcast.12), channel_id=1, replica_groups={{512,528,544,560,576,592,608,624,640,656,672,688,704,720,736,752,768,78..., dimensions={0} | all-to-all | bytes 262144 | tf_op jit(solution)/shard_map/all_to_all | solution.py:255
  54.4 0.3 unfold.1
  54.7 18.5 %all_to_all.21.rows = bf16[8,256,256]{2,1,0:T(8,128)(2,1)S(1)} all-to-all(bf16[8,256,256]{2,1,0:T(8,128)(2,1)S(1)} %unfold.1), channel_id=1, replica_groups={{0,2,4,6,8,10,12,14},{1,3,5,7,9,11,13,15},{16,18,20,22,24,26,28,30},{17..., dimensions={0} | all-to-all | bytes 2097152 | tf_op jit(solution)/shard_map/all_to_all | solution.py:273
  73.2 4.0 %collective-permute-start = (bf16[8,256,256]{2,1,0:T(8,128)(2,1)S(1)}, bf16[8,256,256]{2,1,0:T(8,128)(2,1)S(1)}, u32[]{:S(2)}, u32[]{:S(2)}) collective-permute-start(bf16[8,256,256]{2,1,0:T(8,128)(2,1)S(1)} %all_to_all.21.rows), channel_id=1, source_target_pairs={{0,1},{1,0},{2,3},{3,2},{4,5},{5,4},{6,7},{7,6},{8,9},{9,8},{10,11... | collective-permute-start | bytes 3145736 | tf_op jit(solution)/shard_map/ppermute | solution.py:274
  77.2 0.0 copy-start.2
  77.3 3.1 %project_near.1 = (f32[3,256,256]{2,1,0:T(8,128)S(1)}, bf16[3,8,256,256]{3,2,1,0:T(8,128)(2,1)S(1)}) custom-call(bf16[8,256,256]{2,1,0:T(8,128)(2,1)S(1)} %all_to_all.21.rows, bf16[3,8,2,256,256]{4,3,2,1,0:T(8,128)(2,1)} %bitcast.16), custom_call_target="tpu_custom_call" | custom-call | flops 805306368 | bytes 7864320 | tf_op jit(solution)/shard_map/project_near/pallas_call | solution.py:234
  80.4 0.0 copy-start.5
  80.4 1.1 project_far.1
  81.5 2.7 %collective-permute-start.1 = (bf16[176,256]{1,0:T(8,128)(2,1)S(1)}, bf16[176,256]{1,0:T(8,128)(2,1)S(1)}, u32[]{:S(2)}, u32[]{:S(2)}) collective-permute-start(bf16[176,256]{1,0:T(8,128)(2,1)S(1)} %get-tuple-element.14), channel_id=1, source_target_pairs={{0,32},{32,64},{64,96},{96,128},{128,160},{160,192},{192,224},{224... | collective-permute-start | bytes 270344 | tf_op jit(solution)/shard_map/ppermute | solution.py:298
  84.2 0.5 bands.1
  84.7 1.5 collective-permute-done.1.halo
  86.1 2.0 %mix.1 = bf16[512,128]{1,0:T(8,128)(2,1)} custom-call(bf16[3,256,256]{2,1,0:T(8,128)(2,1)S(1)} %get-tuple-element.13.qkv, bf16[176,256]{1,0:T(8,128)(2,1)S(1)} %collective-permute-done.1.halo, bf16[16,128,256]{2,1,0:T(8,128)(2,1)S(1)} %bands.1, s32[128,128]{1,0:T(8,128)S(1)} %bitcast.14, f32[3,3,256]{2,1,0:T(4,128)S(1)} %copy-done.3, f32[1,256]{1,0:T(1,128)S(1)} %bitcast.15), custom_call_target="tpu_custom_call" | custom-call | flops 536870912 | bytes 2097152 | tf_op jit(solution)/shard_map/mix/pallas_call | solution.py:234
  88.2 25.3 %all-to-all-start.2 = ((bf16[64,8,128]{2,1,0:T(8,128)(2,1)}), bf16[64,8,128]{2,1,0:T(8,128)(2,1)S(1)}, u32[]{:S(2)}, u32[]{:S(2)}) async-start(bf16[64,8,128]{2,1,0:T(8,128)(2,1)} %bitcast.6), calls=%async_computation.2 | async-start | bytes 262144 | tf_op jit(solution)/shard_map/all_to_all | solution.py:255
  113.5 1.5 pick.1
  115.0 3.3 %collective-permute-start.3 = (bf16[8,256,256]{2,1,0:T(8,128)(2,1)}, bf16[8,256,256]{2,1,0:T(8,128)(2,1)S(1)}, u32[]{:S(2)}, u32[]{:S(2)}) collective-permute-start(bf16[8,256,256]{2,1,0:T(8,128)(2,1)} %get-tuple-element.15), channel_id=1, source_target_pairs={{0,1},{1,0},{2,3},{3,2},{4,5},{5,4},{6,7},{7,6},{8,9},{9,8},{10,11... | collective-permute-start | bytes 3145736 | tf_op jit(solution)/shard_map/ppermute | solution.py:303
  118.3 9.2 %all-to-all-done.2 = bf16[64,8,128]{2,1,0:T(8,128)(2,1)S(1)} async-done(((bf16[64,8,128]{2,1,0:T(8,128)(2,1)}), bf16[64,8,128]{2,1,0:T(8,128)(2,1)S(1)}, u32[]{:S(2)}, u32[]{:S(2)}) %all-to-all-start.2) | async-done | bytes 131104 | tf_op jit(solution)/shard_map/all_to_all | solution.py:255
  127.5 3.1 %collective-permute-start.2 = (bf16[512,128]{1,0:T(8,128)(2,1)S(1)}, bf16[512,128]{1,0:T(8,128)(2,1)S(1)}, u32[]{:S(2)}, u32[]{:S(2)}) collective-permute-start(bf16[512,128]{1,0:T(8,128)(2,1)S(1)} %bitcast.9), channel_id=1, source_target_pairs={{0,1},{1,0},{2,3},{3,2},{4,5},{5,4},{6,7},{7,6},{8,9},{9,8},{10,11... | collective-permute-start | bytes 393224 | tf_op jit(solution)/shard_map/ppermute | solution.py:308
  130.6 0.7 out_near.1.near
  131.3 0.3 collective-permute-done.2.packed
  131.6 0.7 out_far.1
  132.3 18.3 %all_to_all.22.terms = bf16[8,256,256]{2,1,0:T(8,128)(2,1)S(1)} all-to-all(bf16[8,256,256]{2,1,0:T(8,128)(2,1)S(1)} %out_far.1), channel_id=1, replica_groups={{0,2,4,6,8,10,12,14},{1,3,5,7,9,11,13,15},{16,18,20,22,24,26,28,30},{17..., dimensions={0} | all-to-all | bytes 2097152 | tf_op jit(solution)/shard_map/all_to_all | solution.py:311
  150.5 0.8 sum.1
  (11 shorter events, 0.0 us)
Async XLA Ops:
  0.0 0.9 copy-start.1
  73.2 7.2 %collective-permute-start = (bf16[8,256,256]{2,1,0:T(8,128)(2,1)S(1)}, bf16[8,256,256]{2,1,0:T(8,128)(2,1)S(1)}, u32[]{:S(2)}, u32[]{:S(2)}) collective-permute-start(bf16[8,256,256]{2,1,0:T(8,128)(2,1)S(1)} %all_to_all.21.rows), channel_id=1, source_target_pairs={{0,1},{1,0},{2,3},{3,2},{4,5},{5,4},{6,7},{7,6},{8,9},{9,8},{10,11... | collective-permute-start | bytes 3145736 | tf_op jit(solution)/shard_map/ppermute | solution.py:274
  77.2 3.2 %copy-start.2 = (s32[16384]{0:T(1024)S(1)}, s32[16384]{0:T(1024)}, u32[]{:S(2)}) copy-start(s32[16384]{0:T(1024)} %param.13) | copy-start | bytes 196612
  77.2 3.2 %copy-start.3 = (f32[3,3,256]{2,1,0:T(4,128)S(1)}, f32[3,3,256]{2,1,0:T(4,128)}, u32[]{:S(2)}) copy-start(f32[3,3,256]{2,1,0:T(4,128)} %short_filter.3) | copy-start | bytes 27652
  80.4 3.8 %copy-start.4 = (bf16[16,128]{1,0:T(8,128)(2,1)S(1)}, bf16[16,128]{1,0:T(8,128)(2,1)}, u32[]{:S(2)}) copy-start(bf16[16,128]{1,0:T(8,128)(2,1)} %filters.1) | copy-start | bytes 12292
  80.4 5.8 %copy-start.5 = (f32[256]{0:T(256)S(1)}, f32[256]{0:T(256)}, u32[]{:S(2)}) copy-start(f32[256]{0:T(256)} %param.11) | copy-start | bytes 3076
  80.4 33.1 %copy-start = (bf16[256,4096]{1,0:T(8,128)(2,1)S(1)}, bf16[256,4096]{1,0:T(8,128)(2,1)}, u32[]{:S(2)}) copy-start(bf16[256,4096]{1,0:T(8,128)(2,1)} %weights.1) | copy-start | bytes 6291460
  81.5 4.6 %collective-permute-start.1 = (bf16[176,256]{1,0:T(8,128)(2,1)S(1)}, bf16[176,256]{1,0:T(8,128)(2,1)S(1)}, u32[]{:S(2)}, u32[]{:S(2)}) collective-permute-start(bf16[176,256]{1,0:T(8,128)(2,1)S(1)} %get-tuple-element.14), channel_id=1, source_target_pairs={{0,32},{32,64},{64,96},{96,128},{128,160},{160,192},{192,224},{224... | collective-permute-start | bytes 270344 | tf_op jit(solution)/shard_map/ppermute | solution.py:298
  88.2 39.4 %all-to-all-start.2 = ((bf16[64,8,128]{2,1,0:T(8,128)(2,1)}), bf16[64,8,128]{2,1,0:T(8,128)(2,1)S(1)}, u32[]{:S(2)}, u32[]{:S(2)}) async-start(bf16[64,8,128]{2,1,0:T(8,128)(2,1)} %bitcast.6), calls=%async_computation.2 | async-start | bytes 262144 | tf_op jit(solution)/shard_map/all_to_all | solution.py:255
  115.0 16.3 %collective-permute-start.3 = (bf16[8,256,256]{2,1,0:T(8,128)(2,1)}, bf16[8,256,256]{2,1,0:T(8,128)(2,1)S(1)}, u32[]{:S(2)}, u32[]{:S(2)}) collective-permute-start(bf16[8,256,256]{2,1,0:T(8,128)(2,1)} %get-tuple-element.15), channel_id=1, source_target_pairs={{0,1},{1,0},{2,3},{3,2},{4,5},{5,4},{6,7},{7,6},{8,9},{9,8},{10,11... | collective-permute-start | bytes 3145736 | tf_op jit(solution)/shard_map/ppermute | solution.py:303
  127.5 4.0 %collective-permute-start.2 = (bf16[512,128]{1,0:T(8,128)(2,1)S(1)}, bf16[512,128]{1,0:T(8,128)(2,1)S(1)}, u32[]{:S(2)}, u32[]{:S(2)}) collective-permute-start(bf16[512,128]{1,0:T(8,128)(2,1)S(1)} %bitcast.9), channel_id=1, source_target_pairs={{0,1},{1,0},{2,3},{3,2},{4,5},{5,4},{6,7},{7,6},{8,9},{9,8},{10,11... | collective-permute-start | bytes 393224 | tf_op jit(solution)/shard_map/ppermute | solution.py:308

commit v5 on v4

--- a/solution.py
+++ b/solution.py
@@ -8,6 +8,7 @@
 BF16 = jnp.bfloat16
 F32 = jnp.float32
 SEQ = 64
+TURN_IN, TURN_OUT = 40, 34
 
 
 def iota(shape, dim):
@@ -31,21 +32,25 @@
     return jnp.where(half == 0, z, SEQ - 1 - z)
 
 
-def peer(chunk):
-    return chunk ^ (SEQ // 2)
-
-
-def fold_source(position):
+def device_at(chunk, turn):
+    return (chunk + turn) & (SEQ - 1)
+
+
+def fold_source(position, turn):
     period, phase = position // (2 * SEQ), position % (2 * SEQ)
     late = phase >= SEQ
     device = jnp.where(late, 2 * SEQ - 1 - phase, phase)
-    return peer(device), 2 * period + late.astype(jnp.int32)
+    return (device - turn) & (SEQ - 1), 2 * period + late.astype(jnp.int32)
+
+
+def member(chip, core):
+    return chip ^ (7 * core)
 
 
 def pack_kernel(tokens, packed):
     shape = (packed.shape[0], tokens.shape[0])
     target, source = iota(shape, 0), iota(shape, 1)
-    wanted = 4 * block_of(peer(target // 8)) + target % 4
+    wanted = 4 * block_of(device_at(target // 8, TURN_IN)) + target % 4
     moved = None
     for part in range(2):
         pick = (source == wanted) & (target // 4 % 2 == part)
@@ -57,7 +62,7 @@
 def unpack(packed, count):
     shape = (count, packed.shape[0])
     target, source = iota(shape, 0), iota(shape, 1)
-    mine = block_of(peer(source // 8)) == target // 4
+    mine = block_of(device_at(source // 8, TURN_OUT)) == target // 4
     halves = []
     for part in range(2):
         pick = mine & (source % 8 == 4 * part + target % 4)
@@ -68,7 +73,7 @@
 def unfold_kernel(received, spread):
     copies, rows, _ = spread.shape
     shape = (rows, received.shape[0])
-    device, slot = fold_source(iota(shape, 0))
+    device, slot = fold_source(iota(shape, 0), TURN_IN)
     column = iota(shape, 1)
     for part in range(2):
         pick = (column == device * 8 + part * 4 + slot).astype(BF16)
@@ -79,7 +84,7 @@
 
 def refold(gated, outgoing):
     shape = (outgoing.shape[0], gated.shape[0])
-    device, slot = fold_source(iota(shape, 1))
+    device, slot = fold_source(iota(shape, 1), TURN_OUT)
     target = iota(shape, 0)
     moved = None
     for part in range(2):
@@ -114,8 +119,8 @@
     return result
 
 
-def join(blocks):
-    return jnp.concatenate([blocks[chip] for chip in range(blocks.shape[0])], axis=1)
+def join(blocks, core):
+    return jnp.concatenate([blocks[member(chip, core)] for chip in range(blocks.shape[0])], axis=1)
 
 
 def project_near_kernel(rows, weights, partial, far_lines, lines, sems):
@@ -128,7 +133,7 @@
     copies.append(pltpu.make_async_copy(weights.at[:, :, 1 - core], far_lines, sems.at[3]))
     for copy in copies:
         copy.start()
-    data = join(rows)
+    data = join(rows, core)
     for part in range(3):
         copies[part].wait()
         partial[part] = dot(data, lines[part].reshape(chips * width, width))
@@ -137,7 +142,7 @@
 
 def project_far_kernel(rows, lines, partial, segments, short_filter, qkv, halo):
     chips, count, width = rows.shape
-    data = join(rows)
+    data = join(rows, 1 - lax.axis_index("chan") % 2)
     for part in range(3):
         total = partial[part] + dot(data, lines[part].reshape(chips * width, width))
         rounded = total.astype(BF16)
@@ -216,14 +221,17 @@
 
 def out_near_kernel(packed, lines, sums):
     rows = unpack(packed, sums.shape[1])
+    core = lax.axis_index("chan") % 2
     for chip in range(sums.shape[0]):
-        sums[chip] = dot(rows, lines[chip])
+        sums[member(chip, core)] = dot(rows, lines[chip])
 
 
 def out_far_kernel(packed, lines, near, sums):
     rows = unpack(packed, sums.shape[1])
+    core = lax.axis_index("chan") % 2
     for chip in range(sums.shape[0]):
-        sums[chip] = (near[chip] + dot(rows, lines[chip])).astype(BF16)
+        place = member(chip, core)
+        sums[place] = (near[place] + dot(rows, lines[chip])).astype(BF16)
 
 
 def kernel(body, name, out_shape, mib, flops, moved, in_place=(), scratch=()):
@@ -249,9 +257,9 @@
     return jax.ShapeDtypeStruct(shape, dtype)
 
 
-def over_seq(packed):
+def over_seq(packed, turn):
     chunks = packed.reshape(SEQ, 8, 128)
-    order = [[peer(chunk) for chunk in range(SEQ)]]
+    order = [[device_at(chunk, turn) for chunk in range(SEQ)]]
     return lax.all_to_all(chunks, "seq", 0, 0, axis_index_groups=order, tiled=True).reshape(8 * SEQ, 128)
 
 
@@ -260,7 +268,7 @@
     width = w_in.shape[0]
     chan_count = lax.axis_size("chan")
     chips = chan_count // 2
-    same_core = [[2 * chip + c for chip in range(chips)] for c in range(2)]
+    same_core = [[2 * member(place, c) + c for place in range(chips)] for c in range(2)]
     partners = [(i, i ^ 1) for i in range(chan_count)]
     holder = {int(k): d for d, k in enumerate([d // 2 if d % 2 == 0 else SEQ - 1 - d // 2 for d in range(SEQ)])}
     ahead = [(holder[k], holder[k + 1]) for k in range(SEQ - 1)]
@@ -269,7 +277,7 @@
     moved = rows * chans * 2
 
     packed = kernel(pack_kernel, "pack", array((8 * SEQ, 128)), 4, 1 << 26, 2 * moved)(tokens)
-    spread = kernel(unfold_kernel, "unfold", array((chips, rows, chans)), 8, 1 << 27, 9 * moved)(over_seq(packed))
+    spread = kernel(unfold_kernel, "unfold", array((chips, rows, chans)), 8, 1 << 27, 9 * moved)(over_seq(packed, TURN_IN))
     near = lax.all_to_all(spread, "chan", 0, 0, axis_index_groups=same_core, tiled=True)
     far = lax.ppermute(near, "chan", partners)
     bands = kernel(band_kernel, "bands", array((mr_filter.shape[0], 128, 256)), 8, 1 << 24, 8 * moved)(mr_filter)
@@ -304,7 +312,7 @@
     outgoing = kernel(
         mix_kernel, "mix", array((8 * SEQ, 128)), 8, 1 << 29, 16 * moved, (), [pltpu.VMEM((rows, chans), BF16)]
     )(qkv, before, bands, segments, short_filter, gain)
-    returned = over_seq(outgoing)
+    returned = over_seq(outgoing, TURN_OUT)
     other = lax.ppermute(returned, "chan", partners)
     sums = kernel(out_near_kernel, "out_near", array(block.shape, F32), 8, work // 3, 16 * moved)(returned, kept)
     sums = kernel(out_far_kernel, "out_far", block, 8, work // 3, 16 * moved)(other, taken, sums)

time: 152 us -> 150 us (0.987)
  blocking collectives: 89.9 us -> 85 us
  starting transfers between devices: 38.4 us -> 40.9 us
    all_to_all x1, blocking collectives: 18.5 us -> 15.9 us  [body(): lax.all_to_all(spread, 'chan', 0, 0, axis_index_groups=same_core, tiled=T...]
    all_to_all x1, blocking collectives: 53.1 us -> 50.9 us  [over_seq(): lax.all_to_all(chunks, 'seq', 0, 0, axis_index_groups=order, tiled=True)]
where the time goes in v5:
time: 150 us; the launch traced here: 149 us
  blocking collectives  85 us (57%)
  starting transfers between devices  40.9 us (27%)
  Pallas kernels  11.2 us (7%)
  waiting for transfers between devices  10.9 us (7%)
    all_to_all x1, blocking collectives, over_seq(): lax.all_to_all(chunks, 'seq', 0, 0, axis_index_groups=order, tiled=True)  50.9 us
    all_to_all x1, starting transfers between devices, over_seq(): lax.all_to_all(chunks, 'seq', 0, 0, axis_index_groups=order, tiled=True)  25.3 us
    all_to_all x1, blocking collectives, body(): lax.all_to_all(sums, 'chan', 0, 0, axis_index_groups=same_core, tiled=True)  18.1 us
    all_to_all x1, blocking collectives, body(): lax.all_to_all(spread, 'chan', 0, 0, axis_index_groups=same_core, tiled=T...  15.9 us
    pallas_call x10, Pallas kernels, call(): pl.pallas_call(body, out_shape=out_shape, in_specs=[anywhere if i in in_p...  11.2 us
    all_to_all x1, waiting for transfers between devices, over_seq(): lax.all_to_all(chunks, 'seq', 0, 0, axis_index_groups=order, tiled=True)  9.25 us
    ppermute x1, starting transfers between devices, body(): far = lax.ppermute(near, 'chan', partners)  5.28 us
    ppermute x1, starting transfers between devices, body(): before = lax.ppermute(halo, 'seq', ahead)  3.5 us
  transfers between devices with their start and end apart: 5, of which 3 were waited for; matrix products, arithmetic and copies ran while one was open for 0% of the time, Pallas kernels for 4%

profile of v5, /device:TPU:1, one launch (start us, length us, event | category | flops | bytes accessed | tf_op | source)
XLA Modules:
  0.0 149.1 jit_solution(8758591269044888127)
XLA Ops:
  0.0 0.9 copy-done.1
  0.9 0.5 pack.1
  1.4 50.9 %all_to_all.20 = bf16[64,8,128]{2,1,0:T(8,128)(2,1)S(1)} all-to-all(bf16[64,8,128]{2,1,0:T(8,128)(2,1)S(1)} %bitcast.12), channel_id=1, replica_groups={{640,656,672,688,704,720,736,752,768,784,800,816,832,848,864,880,896,91..., dimensions={0} | all-to-all | bytes 262144 | tf_op jit(solution)/shard_map/all_to_all | solution.py:263
  52.3 0.3 unfold.1
  52.6 15.9 %all_to_all.21.rows = bf16[8,256,256]{2,1,0:T(8,128)(2,1)S(1)} all-to-all(bf16[8,256,256]{2,1,0:T(8,128)(2,1)S(1)} %unfold.1), channel_id=1, replica_groups={{0,2,4,6,8,10,12,14},{15,13,11,9,7,5,3,1},{16,18,20,22,24,26,28,30},{31..., dimensions={0} | all-to-all | bytes 2097152 | tf_op jit(solution)/shard_map/all_to_all | solution.py:281
  68.6 5.3 %collective-permute-start = (bf16[8,256,256]{2,1,0:T(8,128)(2,1)S(1)}, bf16[8,256,256]{2,1,0:T(8,128)(2,1)S(1)}, u32[]{:S(2)}, u32[]{:S(2)}) collective-permute-start(bf16[8,256,256]{2,1,0:T(8,128)(2,1)S(1)} %all_to_all.21.rows), channel_id=1, source_target_pairs={{0,1},{1,0},{2,3},{3,2},{4,5},{5,4},{6,7},{7,6},{8,9},{9,8},{10,11... | collective-permute-start | bytes 3145736 | tf_op jit(solution)/shard_map/ppermute | solution.py:282
  73.9 0.0 copy-start.3
  73.9 3.1 %project_near.1 = (f32[3,256,256]{2,1,0:T(8,128)S(1)}, bf16[3,8,256,256]{3,2,1,0:T(8,128)(2,1)S(1)}) custom-call(bf16[8,256,256]{2,1,0:T(8,128)(2,1)S(1)} %all_to_all.21.rows, bf16[3,8,2,256,256]{4,3,2,1,0:T(8,128)(2,1)} %bitcast.16), custom_call_target="tpu_custom_call" | custom-call | flops 805306368 | bytes 7864320 | tf_op jit(solution)/shard_map/project_near/pallas_call | solution.py:242
  77.1 0.0 copy-start
  77.1 1.1 project_far.1
  78.1 3.5 %collective-permute-start.1 = (bf16[176,256]{1,0:T(8,128)(2,1)S(1)}, bf16[176,256]{1,0:T(8,128)(2,1)S(1)}, u32[]{:S(2)}, u32[]{:S(2)}) collective-permute-start(bf16[176,256]{1,0:T(8,128)(2,1)S(1)} %get-tuple-element.14), channel_id=1, source_target_pairs={{0,32},{32,64},{64,96},{96,128},{128,160},{160,192},{192,224},{224... | collective-permute-start | bytes 270344 | tf_op jit(solution)/shard_map/ppermute | solution.py:306
  81.7 0.5 bands.1
  82.1 1.5 collective-permute-done.1.halo
  83.6 2.1 %mix.1 = bf16[512,128]{1,0:T(8,128)(2,1)} custom-call(bf16[3,256,256]{2,1,0:T(8,128)(2,1)S(1)} %get-tuple-element.13.qkv, bf16[176,256]{1,0:T(8,128)(2,1)S(1)} %collective-permute-done.1.halo, bf16[16,128,256]{2,1,0:T(8,128)(2,1)S(1)} %bands.1, s32[128,128]{1,0:T(8,128)S(1)} %bitcast.14, f32[3,3,256]{2,1,0:T(4,128)S(1)} %copy-done.3, f32[1,256]{1,0:T(1,128)S(1)} %bitcast.15), custom_call_target="tpu_custom_call" | custom-call | flops 536870912 | bytes 2097152 | tf_op jit(solution)/shard_map/mix/pallas_call | solution.py:242
  85.7 25.3 %all-to-all-start.2 = ((bf16[64,8,128]{2,1,0:T(8,128)(2,1)}), bf16[64,8,128]{2,1,0:T(8,128)(2,1)S(1)}, u32[]{:S(2)}, u32[]{:S(2)}) async-start(bf16[64,8,128]{2,1,0:T(8,128)(2,1)} %bitcast.6), calls=%async_computation.2 | async-start | bytes 262144 | tf_op jit(solution)/shard_map/all_to_all | solution.py:263
  111.0 1.5 pick.1
  112.5 3.3 %collective-permute-start.3 = (bf16[8,256,256]{2,1,0:T(8,128)(2,1)}, bf16[8,256,256]{2,1,0:T(8,128)(2,1)S(1)}, u32[]{:S(2)}, u32[]{:S(2)}) collective-permute-start(bf16[8,256,256]{2,1,0:T(8,128)(2,1)} %get-tuple-element.15), channel_id=1, source_target_pairs={{0,1},{1,0},{2,3},{3,2},{4,5},{5,4},{6,7},{7,6},{8,9},{9,8},{10,11... | collective-permute-start | bytes 3145736 | tf_op jit(solution)/shard_map/ppermute | solution.py:311
  115.8 9.2 %all-to-all-done.2 = bf16[64,8,128]{2,1,0:T(8,128)(2,1)S(1)} async-done(((bf16[64,8,128]{2,1,0:T(8,128)(2,1)}), bf16[64,8,128]{2,1,0:T(8,128)(2,1)S(1)}, u32[]{:S(2)}, u32[]{:S(2)}) %all-to-all-start.2) | async-done | bytes 131104 | tf_op jit(solution)/shard_map/all_to_all | solution.py:263
  125.1 3.5 %collective-permute-start.2 = (bf16[512,128]{1,0:T(8,128)(2,1)S(1)}, bf16[512,128]{1,0:T(8,128)(2,1)S(1)}, u32[]{:S(2)}, u32[]{:S(2)}) collective-permute-start(bf16[512,128]{1,0:T(8,128)(2,1)S(1)} %bitcast.9), channel_id=1, source_target_pairs={{0,1},{1,0},{2,3},{3,2},{4,5},{5,4},{6,7},{7,6},{8,9},{9,8},{10,11... | collective-permute-start | bytes 393224 | tf_op jit(solution)/shard_map/ppermute | solution.py:316
  128.6 0.7 out_near.1.near
  129.3 0.2 collective-permute-done.2.packed
  129.5 0.7 out_far.1
  130.2 18.1 %all_to_all.22.terms = bf16[8,256,256]{2,1,0:T(8,128)(2,1)S(1)} all-to-all(bf16[8,256,256]{2,1,0:T(8,128)(2,1)S(1)} %out_far.1), channel_id=1, replica_groups={{0,2,4,6,8,10,12,14},{15,13,11,9,7,5,3,1},{16,18,20,22,24,26,28,30},{31..., dimensions={0} | all-to-all | bytes 2097152 | tf_op jit(solution)/shard_map/all_to_all | solution.py:319
  148.3 0.8 sum.1
  (11 shorter events, 0.0 us)
Async XLA Ops:
  0.0 0.9 copy-start.1
  68.6 8.5 %collective-permute-start = (bf16[8,256,256]{2,1,0:T(8,128)(2,1)S(1)}, bf16[8,256,256]{2,1,0:T(8,128)(2,1)S(1)}, u32[]{:S(2)}, u32[]{:S(2)}) collective-permute-start(bf16[8,256,256]{2,1,0:T(8,128)(2,1)S(1)} %all_to_all.21.rows), channel_id=1, source_target_pairs={{0,1},{1,0},{2,3},{3,2},{4,5},{5,4},{6,7},{7,6},{8,9},{9,8},{10,11... | collective-permute-start | bytes 3145736 | tf_op jit(solution)/shard_map/ppermute | solution.py:282
  73.9 3.2 %copy-start.2 = (s32[16384]{0:T(1024)S(1)}, s32[16384]{0:T(1024)}, u32[]{:S(2)}) copy-start(s32[16384]{0:T(1024)} %param.13) | copy-start | bytes 196612
  73.9 3.2 %copy-start.3 = (f32[3,3,256]{2,1,0:T(4,128)S(1)}, f32[3,3,256]{2,1,0:T(4,128)}, u32[]{:S(2)}) copy-start(f32[3,3,256]{2,1,0:T(4,128)} %short_filter.3) | copy-start | bytes 27652
  77.0 4.7 %copy-start.4 = (bf16[16,128]{1,0:T(8,128)(2,1)S(1)}, bf16[16,128]{1,0:T(8,128)(2,1)}, u32[]{:S(2)}) copy-start(bf16[16,128]{1,0:T(8,128)(2,1)} %filters.1) | copy-start | bytes 12292
  77.0 6.6 %copy-start.5 = (f32[256]{0:T(256)S(1)}, f32[256]{0:T(256)}, u32[]{:S(2)}) copy-start(f32[256]{0:T(256)} %param.11) | copy-start | bytes 3076
  77.1 33.9 %copy-start = (bf16[256,4096]{1,0:T(8,128)(2,1)S(1)}, bf16[256,4096]{1,0:T(8,128)(2,1)}, u32[]{:S(2)}) copy-start(bf16[256,4096]{1,0:T(8,128)(2,1)} %weights.1) | copy-start | bytes 6291460
  78.1 5.5 %collective-permute-start.1 = (bf16[176,256]{1,0:T(8,128)(2,1)S(1)}, bf16[176,256]{1,0:T(8,128)(2,1)S(1)}, u32[]{:S(2)}, u32[]{:S(2)}) collective-permute-start(bf16[176,256]{1,0:T(8,128)(2,1)S(1)} %get-tuple-element.14), channel_id=1, source_target_pairs={{0,32},{32,64},{64,96},{96,128},{128,160},{160,192},{192,224},{224... | collective-permute-start | bytes 270344 | tf_op jit(solution)/shard_map/ppermute | solution.py:306
  85.7 39.4 %all-to-all-start.2 = ((bf16[64,8,128]{2,1,0:T(8,128)(2,1)}), bf16[64,8,128]{2,1,0:T(8,128)(2,1)S(1)}, u32[]{:S(2)}, u32[]{:S(2)}) async-start(bf16[64,8,128]{2,1,0:T(8,128)(2,1)} %bitcast.6), calls=%async_computation.2 | async-start | bytes 262144 | tf_op jit(solution)/shard_map/all_to_all | solution.py:263
  112.5 16.8 %collective-permute-start.3 = (bf16[8,256,256]{2,1,0:T(8,128)(2,1)}, bf16[8,256,256]{2,1,0:T(8,128)(2,1)S(1)}, u32[]{:S(2)}, u32[]{:S(2)}) collective-permute-start(bf16[8,256,256]{2,1,0:T(8,128)(2,1)} %get-tuple-element.15), channel_id=1, source_target_pairs={{0,1},{1,0},{2,3},{3,2},{4,5},{5,4},{6,7},{7,6},{8,9},{9,8},{10,11... | collective-permute-start | bytes 3145736 | tf_op jit(solution)/shard_map/ppermute | solution.py:311
  125.1 4.5 %collective-permute-start.2 = (bf16[512,128]{1,0:T(8,128)(2,1)S(1)}, bf16[512,128]{1,0:T(8,128)(2,1)S(1)}, u32[]{:S(2)}, u32[]{:S(2)}) collective-permute-start(bf16[512,128]{1,0:T(8,128)(2,1)S(1)} %bitcast.9), channel_id=1, source_target_pairs={{0,1},{1,0},{2,3},{3,2},{4,5},{5,4},{6,7},{7,6},{8,9},{9,8},{10,11... | collective-permute-start | bytes 393224 | tf_op jit(solution)/shard_map/ppermute | solution.py:316

commit v6 on v5

--- a/solution.py
+++ b/solution.py
@@ -49,7 +49,7 @@
 
 def pack_kernel(tokens, packed):
     shape = (packed.shape[0], tokens.shape[0])
-    target, source = iota(shape, 0), iota(shape, 1)
+    target, source = iota((shape[0], 1), 0), iota(shape, 1)
     wanted = 4 * block_of(device_at(target // 8, TURN_IN)) + target % 4
     moved = None
     for part in range(2):
@@ -61,7 +61,7 @@
 
 def unpack(packed, count):
     shape = (count, packed.shape[0])
-    target, source = iota(shape, 0), iota(shape, 1)
+    target, source = iota(shape, 0), iota((1, shape[1]), 1)
     mine = block_of(device_at(source // 8, TURN_OUT)) == target // 4
     halves = []
     for part in range(2):
@@ -73,7 +73,7 @@
 def unfold_kernel(received, spread):
     copies, rows, _ = spread.shape
     shape = (rows, received.shape[0])
-    device, slot = fold_source(iota(shape, 0), TURN_IN)
+    device, slot = fold_source(iota((shape[0], 1), 0), TURN_IN)
     column = iota(shape, 1)
     for part in range(2):
         pick = (column == device * 8 + part * 4 + slot).astype(BF16)
@@ -82,16 +82,12 @@
             spread[copy, :, 128 * part : 128 * (part + 1)] = moved
 
 
-def refold(gated, outgoing):
-    shape = (outgoing.shape[0], gated.shape[0])
-    device, slot = fold_source(iota(shape, 1), TURN_OUT)
+def refold_picks(picks):
+    shape = picks.shape[1:]
+    chunk, slot = fold_source(iota((1, shape[1]), 1), TURN_OUT)
     target = iota(shape, 0)
-    moved = None
-    for part in range(2):
-        pick = (target == device * 8 + part * 4 + slot).astype(BF16)
-        term = dot(pick, gated[:, 128 * part : 128 * (part + 1)])
-        moved = term if moved is None else moved + term
-    outgoing[...] = moved.astype(BF16)
+    for part in range(2):
+        picks[part] = (target == chunk * 8 + part * 4 + slot).astype(BF16)
 
 
 def sum_kernel(terms, mixed):
@@ -147,7 +143,7 @@
         total = partial[part] + dot(data, lines[part].reshape(chips * width, width))
         rounded = total.astype(BF16)
         qkv[part] = rounded
-        halo[128 + 16 * part : 144 + 16 * part, :] = rounded[count - 16 :]
+        halo[128 + 8 * part : 136 + 8 * part, :] = rounded[count - 8 :]
     block = block_of(lax.axis_index("seq"))
     columns = segment_columns(segments, 2 * block, 2)[count - 136 :]
     pair = []
@@ -167,42 +163,85 @@
         bands[group] = pltpu.roll(row, 0, 1, stride=1, stride_axis=0).astype(BF16)
 
 
-def mix_kernel(qkv, halo, bands, segments, short_filter, skip_gain, outgoing, gated_out):
-    seq = block_of(lax.axis_index("seq"))
-    count, chans = gated_out.shape
-    groups = bands.shape[0]
-    size = chans // groups
-    ahead = segment_columns(segments, jnp.maximum(2 * seq - 1, 0), 1)
-    ahead = jnp.where(seq > 0, ahead, -1.0)
-    columns = jnp.concatenate([ahead, segment_columns(segments, 2 * seq, 2)], axis=0)
+def taps_of(short_filter, part):
+    return jnp.stack([short_filter[tap, part : part + 1, :] for tap in range(short_filter.shape[0])])
+
+
+def mask_of(columns, block):
+    own = columns[128 * (block + 1) : 128 * (block + 2)]
+    windows = [jnp.transpose(columns[128 * (block + k) : 128 * (block + k + 1)]) for k in range(2)]
+    return jnp.concatenate([own == window for window in windows], axis=1).astype(F32).astype(BF16)
+
+
+def extended_columns(segments, block):
+    ahead = segment_columns(segments, jnp.maximum(2 * block - 1, 0), 1)
+    ahead = jnp.where(block > 0, ahead, -1.0)
+    return jnp.concatenate([ahead, segment_columns(segments, 2 * block, 2)], axis=0)
+
+
+def banded(bands, window, side, rows, size):
+    depth = window.shape[0]
+    lane_group = iota(window.shape, 1) // size
+    total = None
+    for group in range(128 // size):
+        chosen = jnp.where(lane_group == group, window, jnp.zeros((), BF16))
+        term = dot(bands[side * (128 // size) + group, :rows, :depth], chosen)
+        total = term if total is None else total + term
+    return total
+
+
+def mix_own_kernel(qkv, bands, segments, short_filter, skip_gain, queries, sums, masked, later, picks):
+    _, count, chans = qkv.shape
+    size = chans // bands.shape[0]
+    columns = extended_columns(segments, block_of(lax.axis_index("seq")))
     convolved = []
     for part in range(3):
-        lead = halo[128 + 16 * part : 144 + 16 * part, :].astype(F32)[8:]
-        extended = jnp.concatenate([lead, qkv[part].astype(F32)], axis=0)
-        taps = jnp.stack([short_filter[tap, part : part + 1, :] for tap in range(3)])
-        convolved.append(short_conv(extended, columns[120:], taps, 8))
-    gated = (convolved[1] * convolved[2]).astype(BF16)
-    gated_ext = jnp.concatenate([halo[:128, :], gated], axis=0)
-    lane_group = iota((256, 128), 1) // size
-    for block in range(count // 128):
-        own = columns[128 * (block + 1) : 128 * (block + 2)]
-        masks = [
-            (own == jnp.transpose(columns[128 * (block + k) : 128 * (block + k + 1)]))
-            for k in range(2)
-        ]
-        mask = jnp.concatenate(masks, axis=1).astype(F32).astype(BF16)
-        for side in range(chans // 128):
-            lanes = slice(128 * side, 128 * (side + 1))
-            window = gated_ext[128 * block : 128 * block + 256, lanes]
-            total = jnp.zeros((128, 128), F32)
-            for group in range(128 // size):
-                band = bands[side * (128 // size) + group] * mask
-                chosen = jnp.where(lane_group == group, window, jnp.zeros((), BF16))
-                total = total + dot(band, chosen)
+        extended = jnp.concatenate([jnp.zeros((8, chans), F32), qkv[part].astype(F32)], axis=0)
+        convolved.append(short_conv(extended, columns[120:], taps_of(short_filter, part), 8))
+    queries[...] = convolved[0]
+    product = convolved[1] * convolved[2]
+    gated = jnp.where(iota((count, 1), 0) >= 8, product, 0.0).astype(BF16)
+    for block, target in enumerate((masked, later)):
+        mask = mask_of(columns, block)
+        for group in range(bands.shape[0]):
+            target[group] = bands[group] * mask
+    first = jnp.concatenate([jnp.zeros((128, chans), BF16), gated[:128]], axis=0)
+    for side in range(chans // 128):
+        lanes = slice(128 * side, 128 * (side + 1))
+        for block, (source, window) in enumerate(((masked, first), (later, gated))):
             rows = slice(128 * block, 128 * (block + 1))
             direct = skip_gain[:, lanes] * gated[rows, lanes].astype(F32)
-            gated_out[rows, lanes] = (convolved[0][rows, lanes] * (total + direct)).astype(BF16)
-    refold(gated_out, outgoing)
+            sums[rows, lanes] = banded(source, window[:, lanes], side, 128, size) + direct
+    refold_picks(picks)
+
+
+def mix_rest_kernel(
+    qkv, halo, masked, later, segments, short_filter, skip_gain, queries, sums, picks, outgoing, gated_out
+):
+    _, count, chans = qkv.shape
+    size = chans // masked.shape[0]
+    columns = extended_columns(segments, block_of(lax.axis_index("seq")))[120:136]
+    convolved = []
+    for part in range(3):
+        lead = halo[128 + 8 * part : 136 + 8 * part, :].astype(F32)
+        extended = jnp.concatenate([lead, qkv[part][:16].astype(F32)[:8]], axis=0)
+        convolved.append(short_conv(extended, columns, taps_of(short_filter, part), 8))
+    gated = (convolved[1] * convolved[2]).astype(BF16)
+    window = jnp.concatenate([halo[:128, :], gated, jnp.zeros((120, chans), BF16)], axis=0)
+    query = jnp.concatenate([convolved[0], queries[8:, :]], axis=0)
+    for side in range(chans // 128):
+        lanes = slice(128 * side, 128 * (side + 1))
+        ahead = banded(masked, window[:, lanes], side, 128, size)
+        across = banded(later, window[128:, lanes], side, 8, size)
+        direct = skip_gain[:, lanes] * gated[:, lanes].astype(F32)
+        total = sums[:, lanes] + jnp.concatenate([ahead, across, jnp.zeros((count - 136, 128), F32)], axis=0)
+        total = jnp.concatenate([total[:8] + direct, total[8:]], axis=0)
+        gated_out[:, lanes] = (query[:, lanes] * total).astype(BF16)
+    moved = None
+    for part in range(2):
+        term = dot(picks[part], gated_out[:, 128 * part : 128 * (part + 1)])
+        moved = term if moved is None else moved + term
+    outgoing[...] = moved.astype(BF16)
 
 
 def pick_kernel(weights, given, kept, sems):
@@ -297,7 +336,7 @@
     qkv, halo = kernel(
         project_far_kernel,
         "project_far",
-        (array((3, rows, chans)), array((176, chans))),
+        (array((3, rows, chans)), array((152, chans))),
         8,
         work,
         40 * moved,
@@ -309,9 +348,18 @@
         pick_kernel, "pick", (block, block), 8, 0, 32 * moved, (0,), [pltpu.SemaphoreType.DMA((2, chips))]
     )(w_out)
     taken = lax.ppermute(given, "chan", partners)
+    wide = array((rows, chans), F32)
+    queries, own, masked, later, picks = kernel(
+        mix_own_kernel,
+        "mix_own",
+        (wide, wide, array(bands.shape), array(bands.shape), array((2, 8 * SEQ, rows))),
+        8,
+        1 << 29,
+        32 * moved,
+    )(qkv, bands, segments, short_filter, gain)
     outgoing = kernel(
-        mix_kernel, "mix", array((8 * SEQ, 128)), 8, 1 << 29, 16 * moved, (), [pltpu.VMEM((rows, chans), BF16)]
-    )(qkv, before, bands, segments, short_filter, gain)
+        mix_rest_kernel, "mix_rest", array((8 * SEQ, 128)), 8, 1 << 28, 32 * moved, (), [pltpu.VMEM((rows, chans), BF16)]
+    )(qkv, before, masked, later, segments, short_filter, gain, queries, own, picks)
     returned = over_seq(outgoing, TURN_OUT)
     other = lax.ppermute(returned, "chan", partners)
     sums = kernel(out_near_kernel, "out_near", array(block.shape, F32), 8, work // 3, 16 * moved)(returned, kept)

time: 150 us -> 149 us (level)
    pallas_call x10 -> x11, Pallas kernels: 11.2 us -> 12.3 us  [call(): pl.pallas_call(body, out_shape=out_shape, in_specs=[anywhere if i in in_p...]
  transfers between devices with their start and end apart: 5 -> 5, of which waited for: 3 -> 2; matrix products, arithmetic and copies ran while one was open for 0% -> 0% of each run, Pallas kernels for 4% -> 5%
where the time goes in v6:
time: 149 us; the launch traced here: 148 us
  blocking collectives  85 us (57%)
  starting transfers between devices  40.6 us (27%)
  Pallas kernels  12.3 us (8%)
  waiting for transfers between devices  9.46 us (6%)
    all_to_all x1, blocking collectives, over_seq(): lax.all_to_all(chunks, 'seq', 0, 0, axis_index_groups=order, tiled=True)  50.9 us
    all_to_all x1, starting transfers between devices, over_seq(): lax.all_to_all(chunks, 'seq', 0, 0, axis_index_groups=order, tiled=True)  25 us
    all_to_all x1, blocking collectives, body(): lax.all_to_all(sums, 'chan', 0, 0, axis_index_groups=same_core, tiled=True)  18.1 us
    all_to_all x1, blocking collectives, body(): lax.all_to_all(spread, 'chan', 0, 0, axis_index_groups=same_core, tiled=T...  15.9 us
    pallas_call x11, Pallas kernels, call(): pl.pallas_call(body, out_shape=out_shape, in_specs=[anywhere if i in in_p...  12.3 us
    all_to_all x1, waiting for transfers between devices, over_seq(): lax.all_to_all(chunks, 'seq', 0, 0, axis_index_groups=order, tiled=True)  9.25 us
    ppermute x1, starting transfers between devices, body(): far = lax.ppermute(near, 'chan', partners)  5.28 us
    ppermute x1, starting transfers between devices, body(): before = lax.ppermute(halo, 'seq', ahead)  3.5 us
  transfers between devices with their start and end apart: 5, of which 2 were waited for; matrix products, arithmetic and copies ran while one was open for 0% of the time, Pallas kernels for 5%

profile of v6, /device:TPU:1, one launch (start us, length us, event | category | flops | bytes accessed | tf_op | source)
XLA Modules:
  0.0 148.4 jit_solution(11152319659609288813)
XLA Ops:
  0.0 0.9 copy-done.2
  0.9 0.5 pack.1
  1.4 50.9 %all_to_all.20 = bf16[64,8,128]{2,1,0:T(8,128)(2,1)S(1)} all-to-all(bf16[64,8,128]{2,1,0:T(8,128)(2,1)S(1)} %bitcast.12), channel_id=1, replica_groups={{640,656,672,688,704,720,736,752,768,784,800,816,832,848,864,880,896,91..., dimensions={0} | all-to-all | bytes 262144 | tf_op jit(solution)/shard_map/all_to_all | solution.py:302
  52.3 0.3 unfold.1
  52.6 15.9 %all_to_all.21.rows = bf16[8,256,256]{2,1,0:T(8,128)(2,1)S(1)} all-to-all(bf16[8,256,256]{2,1,0:T(8,128)(2,1)S(1)} %unfold.1), channel_id=1, replica_groups={{0,2,4,6,8,10,12,14},{15,13,11,9,7,5,3,1},{16,18,20,22,24,26,28,30},{31..., dimensions={0} | all-to-all | bytes 2097152 | tf_op jit(solution)/shard_map/all_to_all | solution.py:320
  68.6 5.3 %collective-permute-start = (bf16[8,256,256]{2,1,0:T(8,128)(2,1)S(1)}, bf16[8,256,256]{2,1,0:T(8,128)(2,1)S(1)}, u32[]{:S(2)}, u32[]{:S(2)}) collective-permute-start(bf16[8,256,256]{2,1,0:T(8,128)(2,1)S(1)} %all_to_all.21.rows), channel_id=1, source_target_pairs={{0,1},{1,0},{2,3},{3,2},{4,5},{5,4},{6,7},{7,6},{8,9},{9,8},{10,11... | collective-permute-start | bytes 3145736 | tf_op jit(solution)/shard_map/ppermute | solution.py:321
  73.9 0.0 copy-start.1
  73.9 0.0 copy-start.3
  73.9 3.1 %project_near.1 = (f32[3,256,256]{2,1,0:T(8,128)S(1)}, bf16[3,8,256,256]{3,2,1,0:T(8,128)(2,1)S(1)}) custom-call(bf16[8,256,256]{2,1,0:T(8,128)(2,1)S(1)} %all_to_all.21.rows, bf16[3,8,2,256,256]{4,3,2,1,0:T(8,128)(2,1)} %bitcast.18), custom_call_target="tpu_custom_call" | custom-call | flops 805306368 | bytes 7864320 | tf_op jit(solution)/shard_map/project_near/pallas_call | solution.py:281
  77.1 1.1 project_far.1
  78.1 3.5 %collective-permute-start.1 = (bf16[152,256]{1,0:T(8,128)(2,1)S(1)}, bf16[152,256]{1,0:T(8,128)(2,1)S(1)}, u32[]{:S(2)}, u32[]{:S(2)}) collective-permute-start(bf16[152,256]{1,0:T(8,128)(2,1)S(1)} %get-tuple-element.19), channel_id=1, source_target_pairs={{0,32},{32,64},{64,96},{96,128},{128,160},{160,192},{192,224},{224... | collective-permute-start | bytes 233480 | tf_op jit(solution)/shard_map/ppermute | solution.py:345
  81.7 0.5 bands.1
  82.2 1.5 mix_own.1
  83.6 1.6 %mix_rest.1 = bf16[512,128]{1,0:T(8,128)(2,1)} custom-call(bf16[3,256,256]{2,1,0:T(8,128)(2,1)S(1)} %get-tuple-element.18.qkv, bf16[152,256]{1,0:T(8,128)(2,1)S(1)} %collective-permute-done.1.halo, bf16[16,128,256]{2,1,0:T(8,128)(2,1)S(1)} %get-tuple-element.20.masked, bf16[16,128,256]{2,1,0:T(8,128)(2,1)S(1)} %get-tuple-element.21.later, ...), custom_call_target="tpu_custom_call" | custom-call | flops 268435456 | bytes 4194304 | tf_op jit(solution)/shard_map/mix_rest/pallas_call | solution.py:281
  85.3 25.0 %all-to-all-start.2 = ((bf16[64,8,128]{2,1,0:T(8,128)(2,1)}), bf16[64,8,128]{2,1,0:T(8,128)(2,1)S(1)}, u32[]{:S(2)}, u32[]{:S(2)}) async-start(bf16[64,8,128]{2,1,0:T(8,128)(2,1)} %bitcast.6), calls=%async_computation.2 | async-start | bytes 262144 | tf_op jit(solution)/shard_map/all_to_all | solution.py:302
  110.3 1.5 pick.1
  111.8 3.3 %collective-permute-start.3 = (bf16[8,256,256]{2,1,0:T(8,128)(2,1)}, bf16[8,256,256]{2,1,0:T(8,128)(2,1)S(1)}, u32[]{:S(2)}, u32[]{:S(2)}) collective-permute-start(bf16[8,256,256]{2,1,0:T(8,128)(2,1)} %get-tuple-element.25), channel_id=1, source_target_pairs={{0,1},{1,0},{2,3},{3,2},{4,5},{5,4},{6,7},{7,6},{8,9},{9,8},{10,11... | collective-permute-start | bytes 3145736 | tf_op jit(solution)/shard_map/ppermute | solution.py:350
  115.1 9.2 %all-to-all-done.2 = bf16[64,8,128]{2,1,0:T(8,128)(2,1)S(1)} async-done(((bf16[64,8,128]{2,1,0:T(8,128)(2,1)}), bf16[64,8,128]{2,1,0:T(8,128)(2,1)S(1)}, u32[]{:S(2)}, u32[]{:S(2)}) %all-to-all-start.2) | async-done | bytes 131104 | tf_op jit(solution)/shard_map/all_to_all | solution.py:302
  124.4 3.5 %collective-permute-start.2 = (bf16[512,128]{1,0:T(8,128)(2,1)S(1)}, bf16[512,128]{1,0:T(8,128)(2,1)S(1)}, u32[]{:S(2)}, u32[]{:S(2)}) collective-permute-start(bf16[512,128]{1,0:T(8,128)(2,1)S(1)} %bitcast.9), channel_id=1, source_target_pairs={{0,1},{1,0},{2,3},{3,2},{4,5},{5,4},{6,7},{7,6},{8,9},{9,8},{10,11... | collective-permute-start | bytes 393224 | tf_op jit(solution)/shard_map/ppermute | solution.py:364
  127.8 0.7 out_near.1.near
  128.6 0.2 collective-permute-done.2.packed
  128.8 0.7 out_far.1
  129.5 18.1 %all_to_all.22.terms = bf16[8,256,256]{2,1,0:T(8,128)(2,1)S(1)} all-to-all(bf16[8,256,256]{2,1,0:T(8,128)(2,1)S(1)} %out_far.1), channel_id=1, replica_groups={{0,2,4,6,8,10,12,14},{15,13,11,9,7,5,3,1},{16,18,20,22,24,26,28,30},{31..., dimensions={0} | all-to-all | bytes 2097152 | tf_op jit(solution)/shard_map/all_to_all | solution.py:367
  147.6 0.8 sum.1
  (12 shorter events, 0.0 us)
Async XLA Ops:
  0.0 0.9 copy-start.2
  68.6 8.5 %collective-permute-start = (bf16[8,256,256]{2,1,0:T(8,128)(2,1)S(1)}, bf16[8,256,256]{2,1,0:T(8,128)(2,1)S(1)}, u32[]{:S(2)}, u32[]{:S(2)}) collective-permute-start(bf16[8,256,256]{2,1,0:T(8,128)(2,1)S(1)} %all_to_all.21.rows), channel_id=1, source_target_pairs={{0,1},{1,0},{2,3},{3,2},{4,5},{5,4},{6,7},{7,6},{8,9},{9,8},{10,11... | collective-permute-start | bytes 3145736 | tf_op jit(solution)/shard_map/ppermute | solution.py:321
  73.9 3.2 %copy-start.1 = (s32[16384]{0:T(1024)S(1)}, s32[16384]{0:T(1024)}, u32[]{:S(2)}) copy-start(s32[16384]{0:T(1024)} %param.13) | copy-start | bytes 196612
  73.9 3.2 %copy-start.3 = (f32[3,3,256]{2,1,0:T(4,128)S(1)}, f32[3,3,256]{2,1,0:T(4,128)}, u32[]{:S(2)}) copy-start(f32[3,3,256]{2,1,0:T(4,128)} %short_filter.5) | copy-start | bytes 27652
  77.0 4.6 %copy-start.4 = (bf16[16,128]{1,0:T(8,128)(2,1)S(1)}, bf16[16,128]{1,0:T(8,128)(2,1)}, u32[]{:S(2)}) copy-start(bf16[16,128]{1,0:T(8,128)(2,1)} %filters.1) | copy-start | bytes 12292
  77.0 5.1 %copy-start.5 = (f32[256]{0:T(256)S(1)}, f32[256]{0:T(256)}, u32[]{:S(2)}) copy-start(f32[256]{0:T(256)} %param.11) | copy-start | bytes 3076
  78.1 5.5 %collective-permute-start.1 = (bf16[152,256]{1,0:T(8,128)(2,1)S(1)}, bf16[152,256]{1,0:T(8,128)(2,1)S(1)}, u32[]{:S(2)}, u32[]{:S(2)}) collective-permute-start(bf16[152,256]{1,0:T(8,128)(2,1)S(1)} %get-tuple-element.19), channel_id=1, source_target_pairs={{0,32},{32,64},{64,96},{96,128},{128,160},{160,192},{192,224},{224... | collective-permute-start | bytes 233480 | tf_op jit(solution)/shard_map/ppermute | solution.py:345
  82.1 28.1 %copy-start = (bf16[256,4096]{1,0:T(8,128)(2,1)S(1)}, bf16[256,4096]{1,0:T(8,128)(2,1)}, u32[]{:S(2)}) copy-start(bf16[256,4096]{1,0:T(8,128)(2,1)} %weights.1) | copy-start | bytes 6291460
  85.3 39.1 %all-to-all-start.2 = ((bf16[64,8,128]{2,1,0:T(8,128)(2,1)}), bf16[64,8,128]{2,1,0:T(8,128)(2,1)S(1)}, u32[]{:S(2)}, u32[]{:S(2)}) async-start(bf16[64,8,128]{2,1,0:T(8,128)(2,1)} %bitcast.6), calls=%async_computation.2 | async-start | bytes 262144 | tf_op jit(solution)/shard_map/all_to_all | solution.py:302
  111.8 16.8 %collective-permute-start.3 = (bf16[8,256,256]{2,1,0:T(8,128)(2,1)}, bf16[8,256,256]{2,1,0:T(8,128)(2,1)S(1)}, u32[]{:S(2)}, u32[]{:S(2)}) collective-permute-start(bf16[8,256,256]{2,1,0:T(8,128)(2,1)} %get-tuple-element.25), channel_id=1, source_target_pairs={{0,1},{1,0},{2,3},{3,2},{4,5},{5,4},{6,7},{7,6},{8,9},{9,8},{10,11... | collective-permute-start | bytes 3145736 | tf_op jit(solution)/shard_map/ppermute | solution.py:350
  124.4 4.5 %collective-permute-start.2 = (bf16[512,128]{1,0:T(8,128)(2,1)S(1)}, bf16[512,128]{1,0:T(8,128)(2,1)S(1)}, u32[]{:S(2)}, u32[]{:S(2)}) collective-permute-start(bf16[512,128]{1,0:T(8,128)(2,1)S(1)} %bitcast.9), channel_id=1, source_target_pairs={{0,1},{1,0},{2,3},{3,2},{4,5},{5,4},{6,7},{7,6},{8,9},{9,8},{10,11... | collective-permute-start | bytes 393224 | tf_op jit(solution)/shard_map/ppermute | solution.py:364

commit v7 on v6

--- a/solution.py
+++ b/solution.py
@@ -179,21 +179,24 @@
     return jnp.concatenate([ahead, segment_columns(segments, 2 * block, 2)], axis=0)
 
 
-def banded(bands, window, side, rows, size):
-    depth = window.shape[0]
+def banded(bands, window, side, size):
     lane_group = iota(window.shape, 1) // size
     total = None
     for group in range(128 // size):
         chosen = jnp.where(lane_group == group, window, jnp.zeros((), BF16))
-        term = dot(bands[side * (128 // size) + group, :rows, :depth], chosen)
+        term = dot(bands[side * (128 // size) + group], chosen)
         total = term if total is None else total + term
     return total
 
 
-def mix_own_kernel(qkv, bands, segments, short_filter, skip_gain, queries, sums, masked, later, picks):
+def mix_own_kernel(
+    qkv, bands, segments, short_filter, skip_gain, queries, sums, first, edge, picks, masked
+):
     _, count, chans = qkv.shape
-    size = chans // bands.shape[0]
+    groups = bands.shape[0]
+    size = chans // groups
     columns = extended_columns(segments, block_of(lax.axis_index("seq")))
+    edge[...] = columns[120:136]
     convolved = []
     for part in range(3):
         extended = jnp.concatenate([jnp.zeros((8, chans), F32), qkv[part].astype(F32)], axis=0)
@@ -201,42 +204,46 @@
     queries[...] = convolved[0]
     product = convolved[1] * convolved[2]
     gated = jnp.where(iota((count, 1), 0) >= 8, product, 0.0).astype(BF16)
-    for block, target in enumerate((masked, later)):
-        mask = mask_of(columns, block)
-        for group in range(bands.shape[0]):
-            target[group] = bands[group] * mask
-    first = jnp.concatenate([jnp.zeros((128, chans), BF16), gated[:128]], axis=0)
+    mask = mask_of(columns, 0)
+    for group in range(groups):
+        first[group, :128] = bands[group] * mask
+    mask = mask_of(columns, 1)
+    for group in range(groups):
+        later = bands[group] * mask
+        masked[group] = later
+        first[group, 128:] = jnp.concatenate([jnp.zeros((8, 128), BF16), later[:8, :128]], axis=1)
+    ahead = jnp.concatenate([jnp.zeros((128, chans), BF16), gated[:128]], axis=0)
     for side in range(chans // 128):
         lanes = slice(128 * side, 128 * (side + 1))
-        for block, (source, window) in enumerate(((masked, first), (later, gated))):
+        for block, window in enumerate((ahead, gated)):
             rows = slice(128 * block, 128 * (block + 1))
             direct = skip_gain[:, lanes] * gated[rows, lanes].astype(F32)
-            sums[rows, lanes] = banded(source, window[:, lanes], side, 128, size) + direct
+            source = first.at[:, :128] if block == 0 else masked
+            sums[rows, lanes] = banded(source, window[:, lanes], side, size) + direct
     refold_picks(picks)
 
 
 def mix_rest_kernel(
-    qkv, halo, masked, later, segments, short_filter, skip_gain, queries, sums, picks, outgoing, gated_out
+    qkv, halo, first, edge, short_filter, skip_gain, queries, sums, picks, outgoing, gated_out
 ):
     _, count, chans = qkv.shape
-    size = chans // masked.shape[0]
-    columns = extended_columns(segments, block_of(lax.axis_index("seq")))[120:136]
+    size = chans // first.shape[0]
     convolved = []
     for part in range(3):
         lead = halo[128 + 8 * part : 136 + 8 * part, :].astype(F32)
         extended = jnp.concatenate([lead, qkv[part][:16].astype(F32)[:8]], axis=0)
-        convolved.append(short_conv(extended, columns, taps_of(short_filter, part), 8))
+        convolved.append(short_conv(extended, edge[...], taps_of(short_filter, part), 8))
     gated = (convolved[1] * convolved[2]).astype(BF16)
     window = jnp.concatenate([halo[:128, :], gated, jnp.zeros((120, chans), BF16)], axis=0)
     query = jnp.concatenate([convolved[0], queries[8:, :]], axis=0)
     for side in range(chans // 128):
         lanes = slice(128 * side, 128 * (side + 1))
-        ahead = banded(masked, window[:, lanes], side, 128, size)
-        across = banded(later, window[128:, lanes], side, 8, size)
+        added = banded(first, window[:, lanes], side, size)
         direct = skip_gain[:, lanes] * gated[:, lanes].astype(F32)
-        total = sums[:, lanes] + jnp.concatenate([ahead, across, jnp.zeros((count - 136, 128), F32)], axis=0)
-        total = jnp.concatenate([total[:8] + direct, total[8:]], axis=0)
-        gated_out[:, lanes] = (query[:, lanes] * total).astype(BF16)
+        added = jnp.concatenate(
+            [added[:8] + direct, added[8:], jnp.zeros((count - 136, 128), F32)], axis=0
+        )
+        gated_out[:, lanes] = (query[:, lanes] * (sums[:, lanes] + added)).astype(BF16)
     moved = None
     for part in range(2):
         term = dot(picks[part], gated_out[:, 128 * part : 128 * (part + 1)])
@@ -349,17 +356,20 @@
     )(w_out)
     taken = lax.ppermute(given, "chan", partners)
     wide = array((rows, chans), F32)
-    queries, own, masked, later, picks = kernel(
+    groups = mr_filter.shape[0]
+    queries, own, first, edge, picks = kernel(
         mix_own_kernel,
         "mix_own",
-        (wide, wide, array(bands.shape), array(bands.shape), array((2, 8 * SEQ, rows))),
+        (wide, wide, array((groups, 136, 256)), array((16, 128), F32), array((2, 8 * SEQ, rows))),
         8,
         1 << 29,
         32 * moved,
+        (),
+        [pltpu.VMEM(bands.shape, BF16)],
     )(qkv, bands, segments, short_filter, gain)
     outgoing = kernel(
         mix_rest_kernel, "mix_rest", array((8 * SEQ, 128)), 8, 1 << 28, 32 * moved, (), [pltpu.VMEM((rows, chans), BF16)]
-    )(qkv, before, masked, later, segments, short_filter, gain, queries, own, picks)
+    )(qkv, before, first, edge, short_filter, gain, queries, own, picks)
     returned = over_seq(outgoing, TURN_OUT)
     other = lax.ppermute(returned, "chan", partners)
     sums = kernel(out_near_kernel, "out_near", array(block.shape, F32), 8, work // 3, 16 * moved)(returned, kept)

time: 149 us -> 149 us (level)
  no operation moved by 1% of the time
where the time goes in v7:
time: 149 us; the launch traced here: 148 us
  blocking collectives  85 us (57%)
  starting transfers between devices  40.6 us (27%)
  Pallas kernels  12.1 us (8%)
  waiting for transfers between devices  9.45 us (6%)
    all_to_all x1, blocking collectives, over_seq(): lax.all_to_all(chunks, 'seq', 0, 0, axis_index_groups=order, tiled=True)  50.9 us
    all_to_all x1, starting transfers between devices, over_seq(): lax.all_to_all(chunks, 'seq', 0, 0, axis_index_groups=order, tiled=True)  25 us
    all_to_all x1, blocking collectives, body(): lax.all_to_all(sums, 'chan', 0, 0, axis_index_groups=same_core, tiled=True)  18.2 us
    all_to_all x1, blocking collectives, body(): lax.all_to_all(spread, 'chan', 0, 0, axis_index_groups=same_core, tiled=T...  15.9 us
    pallas_call x11, Pallas kernels, call(): pl.pallas_call(body, out_shape=out_shape, in_specs=[anywhere if i in in_p...  12.1 us
    all_to_all x1, waiting for transfers between devices, over_seq(): lax.all_to_all(chunks, 'seq', 0, 0, axis_index_groups=order, tiled=True)  9.25 us
    ppermute x1, starting transfers between devices, body(): far = lax.ppermute(near, 'chan', partners)  5.28 us
    ppermute x1, starting transfers between devices, body(): before = lax.ppermute(halo, 'seq', ahead)  3.5 us
  transfers between devices with their start and end apart: 5, of which 2 were waited for; matrix products, arithmetic and copies ran while one was open for 0% of the time, Pallas kernels for 5%

profile of v7, /device:TPU:1, one launch (start us, length us, event | category | flops | bytes accessed | tf_op | source)
XLA Modules:
  0.0 148.3 jit_solution(10498455173251862403)
XLA Ops:
  0.0 0.9 copy-done.1
  0.9 0.5 pack.1
  1.4 50.9 %all_to_all.20 = bf16[64,8,128]{2,1,0:T(8,128)(2,1)S(1)} all-to-all(bf16[64,8,128]{2,1,0:T(8,128)(2,1)S(1)} %bitcast.12), channel_id=1, replica_groups={{640,656,672,688,704,720,736,752,768,784,800,816,832,848,864,880,896,91..., dimensions={0} | all-to-all | bytes 262144 | tf_op jit(solution)/shard_map/all_to_all | solution.py:309
  52.3 0.3 unfold.1
  52.6 15.9 %all_to_all.21.rows = bf16[8,256,256]{2,1,0:T(8,128)(2,1)S(1)} all-to-all(bf16[8,256,256]{2,1,0:T(8,128)(2,1)S(1)} %unfold.1), channel_id=1, replica_groups={{0,2,4,6,8,10,12,14},{15,13,11,9,7,5,3,1},{16,18,20,22,24,26,28,30},{31..., dimensions={0} | all-to-all | bytes 2097152 | tf_op jit(solution)/shard_map/all_to_all | solution.py:327
  68.6 5.3 %collective-permute-start = (bf16[8,256,256]{2,1,0:T(8,128)(2,1)S(1)}, bf16[8,256,256]{2,1,0:T(8,128)(2,1)S(1)}, u32[]{:S(2)}, u32[]{:S(2)}) collective-permute-start(bf16[8,256,256]{2,1,0:T(8,128)(2,1)S(1)} %all_to_all.21.rows), channel_id=1, source_target_pairs={{0,1},{1,0},{2,3},{3,2},{4,5},{5,4},{6,7},{7,6},{8,9},{9,8},{10,11... | collective-permute-start | bytes 3145736 | tf_op jit(solution)/shard_map/ppermute | solution.py:328
  73.9 0.0 copy-start.2
  73.9 0.0 copy-start.3
  73.9 3.1 %project_near.1 = (f32[3,256,256]{2,1,0:T(8,128)S(1)}, bf16[3,8,256,256]{3,2,1,0:T(8,128)(2,1)S(1)}) custom-call(bf16[8,256,256]{2,1,0:T(8,128)(2,1)S(1)} %all_to_all.21.rows, bf16[3,8,2,256,256]{4,3,2,1,0:T(8,128)(2,1)} %bitcast.17), custom_call_target="tpu_custom_call" | custom-call | flops 805306368 | bytes 7864320 | tf_op jit(solution)/shard_map/project_near/pallas_call | solution.py:288
  77.1 1.1 project_far.1
  78.1 3.5 %collective-permute-start.1 = (bf16[152,256]{1,0:T(8,128)(2,1)S(1)}, bf16[152,256]{1,0:T(8,128)(2,1)S(1)}, u32[]{:S(2)}, u32[]{:S(2)}) collective-permute-start(bf16[152,256]{1,0:T(8,128)(2,1)S(1)} %get-tuple-element.19), channel_id=1, source_target_pairs={{0,32},{32,64},{64,96},{96,128},{128,160},{160,192},{192,224},{224... | collective-permute-start | bytes 233480 | tf_op jit(solution)/shard_map/ppermute | solution.py:352
  81.7 0.5 bands.1
  82.2 1.4 mix_own.1
  83.6 1.5 mix_rest.1
  85.1 25.0 %all-to-all-start.2 = ((bf16[64,8,128]{2,1,0:T(8,128)(2,1)}), bf16[64,8,128]{2,1,0:T(8,128)(2,1)S(1)}, u32[]{:S(2)}, u32[]{:S(2)}) async-start(bf16[64,8,128]{2,1,0:T(8,128)(2,1)} %bitcast.6), calls=%async_computation.2 | async-start | bytes 262144 | tf_op jit(solution)/shard_map/all_to_all | solution.py:309
  110.1 1.5 pick.1
  111.6 3.3 %collective-permute-start.3 = (bf16[8,256,256]{2,1,0:T(8,128)(2,1)}, bf16[8,256,256]{2,1,0:T(8,128)(2,1)S(1)}, u32[]{:S(2)}, u32[]{:S(2)}) collective-permute-start(bf16[8,256,256]{2,1,0:T(8,128)(2,1)} %get-tuple-element.25), channel_id=1, source_target_pairs={{0,1},{1,0},{2,3},{3,2},{4,5},{5,4},{6,7},{7,6},{8,9},{9,8},{10,11... | collective-permute-start | bytes 3145736 | tf_op jit(solution)/shard_map/ppermute | solution.py:357
  115.0 9.2 %all-to-all-done.2 = bf16[64,8,128]{2,1,0:T(8,128)(2,1)S(1)} async-done(((bf16[64,8,128]{2,1,0:T(8,128)(2,1)}), bf16[64,8,128]{2,1,0:T(8,128)(2,1)S(1)}, u32[]{:S(2)}, u32[]{:S(2)}) %all-to-all-start.2) | async-done | bytes 131104 | tf_op jit(solution)/shard_map/all_to_all | solution.py:309
  124.2 3.5 %collective-permute-start.2 = (bf16[512,128]{1,0:T(8,128)(2,1)S(1)}, bf16[512,128]{1,0:T(8,128)(2,1)S(1)}, u32[]{:S(2)}, u32[]{:S(2)}) collective-permute-start(bf16[512,128]{1,0:T(8,128)(2,1)S(1)} %bitcast.9), channel_id=1, source_target_pairs={{0,1},{1,0},{2,3},{3,2},{4,5},{5,4},{6,7},{7,6},{8,9},{9,8},{10,11... | collective-permute-start | bytes 393224 | tf_op jit(solution)/shard_map/ppermute | solution.py:374
  127.7 0.7 out_near.1.near
  128.5 0.2 collective-permute-done.2.packed
  128.7 0.7 out_far.1
  129.3 18.2 %all_to_all.22.terms = bf16[8,256,256]{2,1,0:T(8,128)(2,1)S(1)} all-to-all(bf16[8,256,256]{2,1,0:T(8,128)(2,1)S(1)} %out_far.1), channel_id=1, replica_groups={{0,2,4,6,8,10,12,14},{15,13,11,9,7,5,3,1},{16,18,20,22,24,26,28,30},{31..., dimensions={0} | all-to-all | bytes 2097152 | tf_op jit(solution)/shard_map/all_to_all | solution.py:377
  147.5 0.8 sum.1
  (12 shorter events, 0.0 us)
Async XLA Ops:
  0.0 0.9 copy-start.1
  68.6 8.4 %collective-permute-start = (bf16[8,256,256]{2,1,0:T(8,128)(2,1)S(1)}, bf16[8,256,256]{2,1,0:T(8,128)(2,1)S(1)}, u32[]{:S(2)}, u32[]{:S(2)}) collective-permute-start(bf16[8,256,256]{2,1,0:T(8,128)(2,1)S(1)} %all_to_all.21.rows), channel_id=1, source_target_pairs={{0,1},{1,0},{2,3},{3,2},{4,5},{5,4},{6,7},{7,6},{8,9},{9,8},{10,11... | collective-permute-start | bytes 3145736 | tf_op jit(solution)/shard_map/ppermute | solution.py:328
  73.9 3.1 %copy-start.2 = (s32[16384]{0:T(1024)S(1)}, s32[16384]{0:T(1024)}, u32[]{:S(2)}) copy-start(s32[16384]{0:T(1024)} %param.13) | copy-start | bytes 196612
  73.9 3.1 %copy-start.3 = (f32[3,3,256]{2,1,0:T(4,128)S(1)}, f32[3,3,256]{2,1,0:T(4,128)}, u32[]{:S(2)}) copy-start(f32[3,3,256]{2,1,0:T(4,128)} %short_filter.5) | copy-start | bytes 27652
  77.0 4.6 %copy-start.4 = (bf16[16,128]{1,0:T(8,128)(2,1)S(1)}, bf16[16,128]{1,0:T(8,128)(2,1)}, u32[]{:S(2)}) copy-start(bf16[16,128]{1,0:T(8,128)(2,1)} %filters.1) | copy-start | bytes 12292
  77.0 5.1 %copy-start.5 = (f32[256]{0:T(256)S(1)}, f32[256]{0:T(256)}, u32[]{:S(2)}) copy-start(f32[256]{0:T(256)} %param.11) | copy-start | bytes 3076
  78.1 5.5 %collective-permute-start.1 = (bf16[152,256]{1,0:T(8,128)(2,1)S(1)}, bf16[152,256]{1,0:T(8,128)(2,1)S(1)}, u32[]{:S(2)}, u32[]{:S(2)}) collective-permute-start(bf16[152,256]{1,0:T(8,128)(2,1)S(1)} %get-tuple-element.19), channel_id=1, source_target_pairs={{0,32},{32,64},{64,96},{96,128},{128,160},{160,192},{192,224},{224... | collective-permute-start | bytes 233480 | tf_op jit(solution)/shard_map/ppermute | solution.py:352
  82.1 28.0 %copy-start = (bf16[256,4096]{1,0:T(8,128)(2,1)S(1)}, bf16[256,4096]{1,0:T(8,128)(2,1)}, u32[]{:S(2)}) copy-start(bf16[256,4096]{1,0:T(8,128)(2,1)} %weights.1) | copy-start | bytes 6291460
  85.1 39.1 %all-to-all-start.2 = ((bf16[64,8,128]{2,1,0:T(8,128)(2,1)}), bf16[64,8,128]{2,1,0:T(8,128)(2,1)S(1)}, u32[]{:S(2)}, u32[]{:S(2)}) async-start(bf16[64,8,128]{2,1,0:T(8,128)(2,1)} %bitcast.6), calls=%async_computation.2 | async-start | bytes 262144 | tf_op jit(solution)/shard_map/all_to_all | solution.py:309
  111.6 16.8 %collective-permute-start.3 = (bf16[8,256,256]{2,1,0:T(8,128)(2,1)}, bf16[8,256,256]{2,1,0:T(8,128)(2,1)S(1)}, u32[]{:S(2)}, u32[]{:S(2)}) collective-permute-start(bf16[8,256,256]{2,1,0:T(8,128)(2,1)} %get-tuple-element.25), channel_id=1, source_target_pairs={{0,1},{1,0},{2,3},{3,2},{4,5},{5,4},{6,7},{7,6},{8,9},{9,8},{10,11... | collective-permute-start | bytes 3145736 | tf_op jit(solution)/shard_map/ppermute | solution.py:357
  124.2 4.5 %collective-permute-start.2 = (bf16[512,128]{1,0:T(8,128)(2,1)S(1)}, bf16[512,128]{1,0:T(8,128)(2,1)S(1)}, u32[]{:S(2)}, u32[]{:S(2)}) collective-permute-start(bf16[512,128]{1,0:T(8,128)(2,1)S(1)} %bitcast.9), channel_id=1, source_target_pairs={{0,1},{1,0},{2,3},{3,2},{4,5},{5,4},{6,7},{7,6},{8,9},{9,8},{10,11... | collective-permute-start | bytes 393224 | tf_op jit(solution)/shard_map/ppermute | solution.py:374

commit v8 on v7

--- a/solution.py
+++ b/solution.py
@@ -8,7 +8,7 @@
 BF16 = jnp.bfloat16
 F32 = jnp.float32
 SEQ = 64
-TURN_IN, TURN_OUT = 40, 34
+TURN_IN, TURN_OUT = 36, 34
 
 
 def iota(shape, dim):

time: 149 us -> 148 us (level)
  starting transfers between devices: 40.6 us -> 36.9 us
  blocking collectives: 85 us -> 88.3 us
    all_to_all x1, blocking collectives: 50.9 us -> 52.7 us  [over_seq(): lax.all_to_all(chunks, 'seq', 0, 0, axis_index_groups=order, tiled=True)]
    ppermute x1, starting transfers between devices: 3.5 us -> 1.67 us  [body(): before = lax.ppermute(halo, 'seq', ahead)]
where the time goes in v8:
time: 148 us
  blocking collectives  88.3 us (60%)
  starting transfers between devices  36.9 us (25%)
  Pallas kernels  12.1 us (8%)
  waiting for transfers between devices  9.45 us (6%)
    all_to_all x1, blocking collectives, over_seq(): lax.all_to_all(chunks, 'seq', 0, 0, axis_index_groups=order, tiled=True)  52.7 us
    all_to_all x1, starting transfers between devices, over_seq(): lax.all_to_all(chunks, 'seq', 0, 0, axis_index_groups=order, tiled=True)  24.6 us
    all_to_all x1, blocking collectives, body(): lax.all_to_all(sums, 'chan', 0, 0, axis_index_groups=same_core, tiled=True)  18.3 us
    all_to_all x1, blocking collectives, body(): lax.all_to_all(spread, 'chan', 0, 0, axis_index_groups=same_core, tiled=T...  17.3 us
    pallas_call x11, Pallas kernels, call(): pl.pallas_call(body, out_shape=out_shape, in_specs=[anywhere if i in in_p...  12.1 us
    all_to_all x1, waiting for transfers between devices, over_seq(): lax.all_to_all(chunks, 'seq', 0, 0, axis_index_groups=order, tiled=True)  9.25 us
    ppermute x1, starting transfers between devices, body(): far = lax.ppermute(near, 'chan', partners)  3.82 us
    ppermute x1, starting transfers between devices, body(): other = lax.ppermute(returned, 'chan', partners)  3.48 us
  transfers between devices with their start and end apart: 5, of which 2 were waited for; matrix products, arithmetic and copies ran while one was open for 0% of the time, Pallas kernels for 5%

profile of v8, /device:TPU:1, one launch (start us, length us, event | category | flops | bytes accessed | tf_op | source)
XLA Modules:
  0.0 147.9 jit_solution(2145354659695267240)
XLA Ops:
  0.0 0.9 copy-done.1
  0.9 0.5 pack.1
  1.4 52.7 %all_to_all.20 = bf16[64,8,128]{2,1,0:T(8,128)(2,1)S(1)} all-to-all(bf16[64,8,128]{2,1,0:T(8,128)(2,1)S(1)} %bitcast.12), channel_id=1, replica_groups={{576,592,608,624,640,656,672,688,704,720,736,752,768,784,800,816,832,84..., dimensions={0} | all-to-all | bytes 262144 | tf_op jit(solution)/shard_map/all_to_all | solution.py:309
  54.1 0.3 unfold.1
  54.5 17.3 %all_to_all.21.rows = bf16[8,256,256]{2,1,0:T(8,128)(2,1)S(1)} all-to-all(bf16[8,256,256]{2,1,0:T(8,128)(2,1)S(1)} %unfold.1), channel_id=1, replica_groups={{0,2,4,6,8,10,12,14},{15,13,11,9,7,5,3,1},{16,18,20,22,24,26,28,30},{31..., dimensions={0} | all-to-all | bytes 2097152 | tf_op jit(solution)/shard_map/all_to_all | solution.py:327
  71.7 3.8 %collective-permute-start = (bf16[8,256,256]{2,1,0:T(8,128)(2,1)S(1)}, bf16[8,256,256]{2,1,0:T(8,128)(2,1)S(1)}, u32[]{:S(2)}, u32[]{:S(2)}) collective-permute-start(bf16[8,256,256]{2,1,0:T(8,128)(2,1)S(1)} %all_to_all.21.rows), channel_id=1, source_target_pairs={{0,1},{1,0},{2,3},{3,2},{4,5},{5,4},{6,7},{7,6},{8,9},{9,8},{10,11... | collective-permute-start | bytes 3145736 | tf_op jit(solution)/shard_map/ppermute | solution.py:328
  75.6 3.1 %project_near.1 = (f32[3,256,256]{2,1,0:T(8,128)S(1)}, bf16[3,8,256,256]{3,2,1,0:T(8,128)(2,1)S(1)}) custom-call(bf16[8,256,256]{2,1,0:T(8,128)(2,1)S(1)} %all_to_all.21.rows, bf16[3,8,2,256,256]{4,3,2,1,0:T(8,128)(2,1)} %bitcast.17), custom_call_target="tpu_custom_call" | custom-call | flops 805306368 | bytes 7864320 | tf_op jit(solution)/shard_map/project_near/pallas_call | solution.py:288
  78.7 0.0 copy-start.5
  78.7 1.1 project_far.1
  79.8 1.7 %collective-permute-start.1 = (bf16[152,256]{1,0:T(8,128)(2,1)S(1)}, bf16[152,256]{1,0:T(8,128)(2,1)S(1)}, u32[]{:S(2)}, u32[]{:S(2)}) collective-permute-start(bf16[152,256]{1,0:T(8,128)(2,1)S(1)} %get-tuple-element.19), channel_id=1, source_target_pairs={{0,32},{32,64},{64,96},{96,128},{128,160},{160,192},{192,224},{224... | collective-permute-start | bytes 233480 | tf_op jit(solution)/shard_map/ppermute | solution.py:352
  81.5 0.5 bands.1
  82.0 0.0 copy-start
  82.0 1.4 mix_own.1
  83.5 1.5 mix_rest.1
  84.9 24.6 %all-to-all-start.2 = ((bf16[64,8,128]{2,1,0:T(8,128)(2,1)}), bf16[64,8,128]{2,1,0:T(8,128)(2,1)S(1)}, u32[]{:S(2)}, u32[]{:S(2)}) async-start(bf16[64,8,128]{2,1,0:T(8,128)(2,1)} %bitcast.6), calls=%async_computation.2 | async-start | bytes 262144 | tf_op jit(solution)/shard_map/all_to_all | solution.py:309
  109.5 1.5 pick.1
  111.0 3.3 %collective-permute-start.3 = (bf16[8,256,256]{2,1,0:T(8,128)(2,1)}, bf16[8,256,256]{2,1,0:T(8,128)(2,1)S(1)}, u32[]{:S(2)}, u32[]{:S(2)}) collective-permute-start(bf16[8,256,256]{2,1,0:T(8,128)(2,1)} %get-tuple-element.25), channel_id=1, source_target_pairs={{0,1},{1,0},{2,3},{3,2},{4,5},{5,4},{6,7},{7,6},{8,9},{9,8},{10,11... | collective-permute-start | bytes 3145736 | tf_op jit(solution)/shard_map/ppermute | solution.py:357
  114.4 9.2 %all-to-all-done.2 = bf16[64,8,128]{2,1,0:T(8,128)(2,1)S(1)} async-done(((bf16[64,8,128]{2,1,0:T(8,128)(2,1)}), bf16[64,8,128]{2,1,0:T(8,128)(2,1)S(1)}, u32[]{:S(2)}, u32[]{:S(2)}) %all-to-all-start.2) | async-done | bytes 131104 | tf_op jit(solution)/shard_map/all_to_all | solution.py:309
  123.6 3.5 %collective-permute-start.2 = (bf16[512,128]{1,0:T(8,128)(2,1)S(1)}, bf16[512,128]{1,0:T(8,128)(2,1)S(1)}, u32[]{:S(2)}, u32[]{:S(2)}) collective-permute-start(bf16[512,128]{1,0:T(8,128)(2,1)S(1)} %bitcast.9), channel_id=1, source_target_pairs={{0,1},{1,0},{2,3},{3,2},{4,5},{5,4},{6,7},{7,6},{8,9},{9,8},{10,11... | collective-permute-start | bytes 393224 | tf_op jit(solution)/shard_map/ppermute | solution.py:374
  127.1 0.8 out_near.1.near
  127.9 0.2 collective-permute-done.2.packed
  128.1 0.7 out_far.1
  128.8 18.3 %all_to_all.22.terms = bf16[8,256,256]{2,1,0:T(8,128)(2,1)S(1)} all-to-all(bf16[8,256,256]{2,1,0:T(8,128)(2,1)S(1)} %out_far.1), channel_id=1, replica_groups={{0,2,4,6,8,10,12,14},{15,13,11,9,7,5,3,1},{16,18,20,22,24,26,28,30},{31..., dimensions={0} | all-to-all | bytes 2097152 | tf_op jit(solution)/shard_map/all_to_all | solution.py:377
  147.1 0.8 sum.1
  (12 shorter events, 0.0 us)
Async XLA Ops:
  0.0 0.9 copy-start.1
  71.7 7.0 %collective-permute-start = (bf16[8,256,256]{2,1,0:T(8,128)(2,1)S(1)}, bf16[8,256,256]{2,1,0:T(8,128)(2,1)S(1)}, u32[]{:S(2)}, u32[]{:S(2)}) collective-permute-start(bf16[8,256,256]{2,1,0:T(8,128)(2,1)S(1)} %all_to_all.21.rows), channel_id=1, source_target_pairs={{0,1},{1,0},{2,3},{3,2},{4,5},{5,4},{6,7},{7,6},{8,9},{9,8},{10,11... | collective-permute-start | bytes 3145736 | tf_op jit(solution)/shard_map/ppermute | solution.py:328
  75.5 3.1 %copy-start.2 = (s32[16384]{0:T(1024)S(1)}, s32[16384]{0:T(1024)}, u32[]{:S(2)}) copy-start(s32[16384]{0:T(1024)} %param.13) | copy-start | bytes 196612
  75.6 3.1 %copy-start.3 = (f32[3,3,256]{2,1,0:T(4,128)S(1)}, f32[3,3,256]{2,1,0:T(4,128)}, u32[]{:S(2)}) copy-start(f32[3,3,256]{2,1,0:T(4,128)} %short_filter.5) | copy-start | bytes 27652
  78.7 2.8 %copy-start.4 = (bf16[16,128]{1,0:T(8,128)(2,1)S(1)}, bf16[16,128]{1,0:T(8,128)(2,1)}, u32[]{:S(2)}) copy-start(bf16[16,128]{1,0:T(8,128)(2,1)} %filters.1) | copy-start | bytes 12292
  78.7 3.3 %copy-start.5 = (f32[256]{0:T(256)S(1)}, f32[256]{0:T(256)}, u32[]{:S(2)}) copy-start(f32[256]{0:T(256)} %param.11) | copy-start | bytes 3076
  79.8 3.6 %collective-permute-start.1 = (bf16[152,256]{1,0:T(8,128)(2,1)S(1)}, bf16[152,256]{1,0:T(8,128)(2,1)S(1)}, u32[]{:S(2)}, u32[]{:S(2)}) collective-permute-start(bf16[152,256]{1,0:T(8,128)(2,1)S(1)} %get-tuple-element.19), channel_id=1, source_target_pairs={{0,32},{32,64},{64,96},{96,128},{128,160},{160,192},{192,224},{224... | collective-permute-start | bytes 233480 | tf_op jit(solution)/shard_map/ppermute | solution.py:352
  82.0 27.5 %copy-start = (bf16[256,4096]{1,0:T(8,128)(2,1)S(1)}, bf16[256,4096]{1,0:T(8,128)(2,1)}, u32[]{:S(2)}) copy-start(bf16[256,4096]{1,0:T(8,128)(2,1)} %weights.1) | copy-start | bytes 6291460
  84.9 38.7 %all-to-all-start.2 = ((bf16[64,8,128]{2,1,0:T(8,128)(2,1)}), bf16[64,8,128]{2,1,0:T(8,128)(2,1)S(1)}, u32[]{:S(2)}, u32[]{:S(2)}) async-start(bf16[64,8,128]{2,1,0:T(8,128)(2,1)} %bitcast.6), calls=%async_computation.2 | async-start | bytes 262144 | tf_op jit(solution)/shard_map/all_to_all | solution.py:309
  111.0 16.8 %collective-permute-start.3 = (bf16[8,256,256]{2,1,0:T(8,128)(2,1)}, bf16[8,256,256]{2,1,0:T(8,128)(2,1)S(1)}, u32[]{:S(2)}, u32[]{:S(2)}) collective-permute-start(bf16[8,256,256]{2,1,0:T(8,128)(2,1)} %get-tuple-element.25), channel_id=1, source_target_pairs={{0,1},{1,0},{2,3},{3,2},{4,5},{5,4},{6,7},{7,6},{8,9},{9,8},{10,11... | collective-permute-start | bytes 3145736 | tf_op jit(solution)/shard_map/ppermute | solution.py:357
  123.6 4.5 %collective-permute-start.2 = (bf16[512,128]{1,0:T(8,128)(2,1)S(1)}, bf16[512,128]{1,0:T(8,128)(2,1)S(1)}, u32[]{:S(2)}, u32[]{:S(2)}) collective-permute-start(bf16[512,128]{1,0:T(8,128)(2,1)S(1)} %bitcast.9), channel_id=1, source_target_pairs={{0,1},{1,0},{2,3},{3,2},{4,5},{5,4},{6,7},{7,6},{8,9},{9,8},{10,11... | collective-permute-start | bytes 393224 | tf_op jit(solution)/shard_map/ppermute | solution.py:374
